TPU v7x, 32 devices: a whole 2x2x4 slice. The times are simulated.
32 devices in a mesh: groups: 2 (over x), seq: 16 (over z, y, core).
Axes of the slice: x: 2, y: 2, z: 4, core: 2. Of those that a mesh axis runs over, the one named last changes fastest.
Arguments:
- x_true: float32 [3, 4096], P(None, ('groups', 'seq')), parts along dimension 1, may hold values from -96 to 96
- noise: float32 [8, 3, 2048], P('groups', None, 'seq'), parts along dimension 0, may hold values from -6 to 6
- noise_level: int32 [8], P('groups'), parts along dimension 0, may hold values from 0 to 199
- atom_single: bfloat16 [4096, 128], P(('groups', 'seq')), parts along dimension 0, may hold values from -6 to 6
- atom_token: int32 [4096], P(('groups', 'seq')), parts along dimension 0, may hold values from 0 to 255, as said below
- window_edges: int32 [128, 2], P(('groups', 'seq')), parts along dimension 0, may hold values from 0 to 2048, as said below
- atom_pair_bias: float32 [128, 4, 32, 128], P(('groups', 'seq')), parts along dimension 0, may hold values from -6 to 300
- token_single: float32 [512, 768], P(('groups', 'seq')), parts along dimension 0, may hold values from -6 to 6
- pair_bias: float32 [32, 256, 256], P('groups', 'seq'), parts along dimension 0, may hold values from -6 to 300
- w_coord: float32 [3, 128], replicated, may hold values from -3.5 to 3.5
- w_atom_qkv: bfloat16 [4, 128, 384], replicated, may hold values from -0.5 to 0.5
- w_atom_out: bfloat16 [4, 128, 128], replicated, may hold values from -0.5 to 0.5
- w_atom_up: bfloat16 [4, 128, 512], replicated, may hold values from -0.5 to 0.5
- w_atom_down: bfloat16 [4, 256, 128], replicated, may hold values from -0.375 to 0.375
- w_pool: bfloat16 [128, 768], replicated, may hold values from -0.5 to 0.5
- w_token_qkv: bfloat16 [768, 2304], replicated, may hold values from -0.21875 to 0.21875
- w_token_out: bfloat16 [768, 768], replicated, may hold values from -0.21875 to 0.21875
- w_back: bfloat16 [768, 128], replicated, may hold values from -0.21875 to 0.21875
- w_final: bfloat16 [3, 128], replicated, may hold values from -0.5 to 0.5
Outputs:
- denoised: float32 [8, 3, 2048], P('groups', None, 'seq'), parts along dimension 0
- token_state: float32 [8, 256, 768], P('groups', 'seq'), parts along dimension 0
There are 2 independent parts, one for each index of `groups`. A program takes and returns all parts, laid end to end along the dimension named above; an argument that names none is the same for every part. Nothing has to cross between parts.
Inputs may be any that keep to these rules, and one draw needn't show every extreme that they name: `atom_token`: never falls along the atoms; every token has one or more atoms; the atoms of token t lie at or after atom 128 * (t // 16) - 48 and before atom 128 * (t // 16) + 128 + 128 * 3 // 8, so the atoms of shard d of the atoms name tokens of token shards d - 1, d and d + 1 only. For block b: max(0, 32 * b - 48) <= window_edges[b, 0] <= max(0, 32 * b - 48 + 48 // 3) and min(2048, 32 * b + 80 - 48 // 3) <= window_edges[b, 1] <= min(2048, 32 * b + 80).
All inputs are finite; a program needn't handle non-finite values.
Results may differ from a plain program's by a relative error of at most 0.008.
Values may be sent and summed in bfloat16 or wider, within the bound.
A program may use at most 128 MiB of HBM per device.

v0:
```python
import functools

import jax
import jax.numpy as jnp
from jax import lax
from jax.experimental import pallas as pl
from jax.experimental.pallas import tpu as pltpu
from jax.sharding import PartitionSpec as P

QUERY_BLOCK = 32
KEY_WINDOW = 128
ENC_LAYERS = 2
LEVELS = 200
RIM = 48
LAYERS = 4
GROUPS = 2

EPS = 1e-05
SIGMA_DATA = 16.0
MESH = pl.DeviceIdType.MESH
F32 = jnp.float32
BF16 = jnp.bfloat16
LAST = (((1,), (1,)), ((), ()))
FIRST = (((0,), (0,)), ((), ()))


def normed(values):
    centred = values - jnp.mean(values, -1, keepdims=True)
    spread = jnp.mean(centred * centred, -1, keepdims=True)
    return centred * lax.rsqrt(spread + EPS)


def dot(a, b):
    return jnp.dot(a, b, preferred_element_type=F32)


def remote(src, dst, send, recv, target):
    return pltpu.make_async_remote_copy(
        src_ref=src,
        dst_ref=dst,
        send_sem=send,
        recv_sem=recv,
        device_id={"seq": target},
        device_id_type=MESH,
    )


def plan(n, heads, samples):
    per = heads * samples // n
    gs = samples // GROUPS
    pack = 2 if per % 2 == 0 else 1
    waves = GROUPS if per == samples and gs == pack else 1
    return per, pack, waves, per // pack // waves


def kernel(
    n,
    level_ref,
    edges_ref,
    x_true_ref,
    noise_ref,
    single_ref,
    atom_token_ref,
    bias_hbm,
    token_single_hbm,
    pair_hbm,
    w_coord_ref,
    w_qkv_hbm,
    w_out_hbm,
    w_up_hbm,
    w_down_hbm,
    w_pool_hbm,
    w_tqkv_hbm,
    w_tout_hbm,
    w_back_hbm,
    w_final_ref,
    denoised_ref,
    state_ref,
    stream,
    kv,
    queries,
    masked_bias,
    counts,
    own_sum,
    psend,
    precv,
    token_in,
    items,
    got,
    pair_buf,
    outs,
    returned,
    back,
    w_tqkv,
    w_tout,
    bias_ref,
    token_single_ref,
    w_qkv_ref,
    w_out_ref,
    w_up_ref,
    w_down_ref,
    w_pool_ref,
    w_back_ref,
    w_sem,
    late_sem,
    halo_send,
    halo_recv,
    count_send,
    count_recv,
    pool_send,
    pool_recv,
    pair_send,
    pair_recv,
    item_send,
    item_recv,
    out_send,
    out_recv,
    back_send,
    back_recv,
):
    samples = noise_ref.shape[1]
    atom_rows, width = single_ref.shape
    token_rows, channels = token_single_ref.shape
    blocks, atom_heads = bias_ref.shape[:2]
    atom_head = width // atom_heads
    heads = pair_hbm.shape[0]
    head_size = channels // heads
    tokens = n * token_rows
    gs = samples // GROUPS
    per, pack, waves, units = plan(n, heads, samples)
    wave_samples = samples // waves
    wave_rows = wave_samples * token_rows

    me = lax.axis_index("seq")
    right = lax.rem(me + 1, n)
    left = lax.rem(me + n - 1, n)
    has_left = me > 0
    has_right = me < n - 1

    barrier = pltpu.get_barrier_semaphore()

    def greet(k, c):
        pl.semaphore_signal(
            barrier, inc=1, device_id={"seq": lax.rem(me + k, n)}, device_id_type=MESH
        )
        return c

    lax.fori_loop(1, n, greet, 0)
    load_tqkv = pltpu.make_async_copy(w_tqkv_hbm, w_tqkv, w_sem.at[0])
    load_tout = pltpu.make_async_copy(w_tout_hbm, w_tout, w_sem.at[1])
    late = {}
    for slot, (name, src, dst) in enumerate(
        (
            ("qkv", w_qkv_hbm, w_qkv_ref),
            ("bias", bias_hbm, bias_ref),
            ("out", w_out_hbm, w_out_ref),
            ("up", w_up_hbm, w_up_ref),
            ("down", w_down_hbm, w_down_ref),
            ("pool", w_pool_hbm, w_pool_ref),
            ("single", token_single_hbm, token_single_ref),
            ("back", w_back_hbm, w_back_ref),
        )
    ):
        late[name] = pltpu.make_async_copy(src, dst, late_sem.at[slot])
        late[name].start()
    load_tqkv.start()
    load_tout.start()
    own_head = (me * per) // samples
    own_pair = pltpu.make_async_copy(pair_hbm.at[own_head], pair_buf.at[me], w_sem.at[2])
    own_pair.start()

    upper_root = 160.0 ** (1.0 / 7.0)
    lower_root = 0.0004 ** (1.0 / 7.0)

    def sigma_of(s):
        level = jnp.full((1, atom_rows), level_ref[s], jnp.int32).astype(F32)
        base = upper_root + level / (LEVELS - 1) * (lower_root - upper_root)
        square = base * base
        sigma = SIGMA_DATA * (square * square * square * base)
        return sigma, sigma * sigma + SIGMA_DATA * SIGMA_DATA

    def noisy_of(s, sigma):
        noise = jnp.concatenate([noise_ref[c, pl.ds(s, 1), :] for c in range(3)], axis=0)
        return x_true_ref[...] + sigma * noise

    scaled = []
    for s in range(samples):
        sigma, total = sigma_of(s)
        scaled.append(noisy_of(s, sigma) * lax.rsqrt(total))
    spare = atom_rows - 3 * samples
    columns = jnp.transpose(
        jnp.concatenate(scaled + [jnp.zeros((spare, atom_rows), F32)], axis=0)
    )
    single = single_ref[...].astype(F32)
    for s in range(samples):
        value = single
        for c in range(3):
            at = 3 * s + c
            value = value + columns[:, at : at + 1] * w_coord_ref[c : c + 1, :]
        stream[s // gs, pl.ds((s % gs) * atom_rows, atom_rows), :] = value

    relative = atom_token_ref[...] - (me - 1) * token_rows
    selector = (
        lax.broadcasted_iota(jnp.int32, (3 * token_rows, atom_rows), 0) == relative
    ).astype(F32)
    sel = selector.astype(BF16)
    counted = jnp.broadcast_to(jnp.sum(selector, 1, keepdims=True), (3 * token_rows, 128))
    for j in range(3):
        counts[j] = counted[j * token_rows : (j + 1) * token_rows].astype(BF16)

    def exchange(to_right, to_left, begin):
        if begin:

            @pl.when(has_right)
            def _():
                to_right.start()

            @pl.when(has_left)
            def _():
                to_left.start()

        else:

            @pl.when(has_left)
            def _():
                to_right.wait_recv()
                to_left.wait_send()

            @pl.when(has_right)
            def _():
                to_left.wait_recv()
                to_right.wait_send()

    def halo(layer, g):
        return (
            remote(
                kv.at[layer, g, :, pl.ds(atom_rows, RIM), :],
                kv.at[layer, g, :, pl.ds(0, RIM), :],
                halo_send.at[layer, g, 0],
                halo_recv.at[layer, g, 0],
                right,
            ),
            remote(
                kv.at[layer, g, :, pl.ds(RIM, RIM), :],
                kv.at[layer, g, :, pl.ds(RIM + atom_rows, RIM), :],
                halo_send.at[layer, g, 1],
                halo_recv.at[layer, g, 1],
                left,
            ),
        )

    def project(layer, g):
        normal_in = normed(stream[g]).astype(BF16)
        key_value = dot(normal_in, w_qkv_ref[layer, :, width:]).astype(BF16)
        for i in range(gs):
            kv[layer, g, i, RIM : RIM + atom_rows, :] = key_value[
                i * atom_rows : (i + 1) * atom_rows
            ]
        queries[g] = dot(normal_in, w_qkv_ref[layer, :, :width]).astype(BF16)

    def send_halo(layer, g):
        exchange(*halo(layer, g), True)

    stacked = atom_heads * QUERY_BLOCK
    row_head = lax.broadcasted_iota(jnp.int32, (stacked, width), 0) // QUERY_BLOCK
    lane_head = lax.broadcasted_iota(jnp.int32, (stacked, width), 1) // atom_head
    own_lanes = row_head == lane_head
    few_lanes = lane_head[:QUERY_BLOCK]
    scale = atom_head ** (-0.5)
    ones = jnp.ones((KEY_WINDOW, width), BF16)

    def attend(layer, g):
        exchange(*halo(layer, g), False)
        mixed = []
        pairs = [(i, b) for i in range(gs) for b in range(blocks)]
        for start in range(0, len(pairs), 8):
            part = pairs[start : start + 8]
            scores = []
            for i, b in part:
                q = queries[g, pl.ds(i * atom_rows + b * QUERY_BLOCK, QUERY_BLOCK), :]
                q = jnp.concatenate([q] * atom_heads, axis=0)
                q = jnp.where(own_lanes, q, jnp.zeros_like(q))
                key_win = kv[layer, g, i, QUERY_BLOCK * b : QUERY_BLOCK * b + KEY_WINDOW, :width]
                score = lax.dot_general(q, key_win, LAST, preferred_element_type=F32)
                scores.append(score * scale + masked_bias[b])
            tops = [jnp.max(score, -1, keepdims=True) for score in scores]
            expos = [jnp.exp(score - top).astype(BF16) for score, top in zip(scores, tops)]
            sums = []
            for (i, b), expo in zip(part, expos):
                value_win = kv[layer, g, i, QUERY_BLOCK * b : QUERY_BLOCK * b + KEY_WINDOW, width:]
                sums.append(dot(expo, jnp.concatenate([value_win, ones], axis=1)))
            for both in sums:
                picked = both[:QUERY_BLOCK]
                number, below = picked[:, :width], picked[:, width:]
                for h in range(1, atom_heads):
                    rows = both[h * QUERY_BLOCK : (h + 1) * QUERY_BLOCK]
                    number = jnp.where(few_lanes == h, rows[:, :width], number)
                    below = jnp.where(few_lanes == h, rows[:, width:], below)
                mixed.append((number / below).astype(BF16))
        mixed = jnp.concatenate(mixed, axis=0)
        value = stream[g] + dot(mixed, w_out_ref[layer])
        normal_mid = normed(value).astype(BF16)
        gated = dot(normal_mid, w_up_ref[layer])
        gate = gated[:, : 2 * width]
        hidden = (gate / (1.0 + jnp.exp(-gate)) * gated[:, 2 * width :]).astype(BF16)
        value = value + dot(hidden, w_down_ref[layer])
        stream[g] = value
        return value

    def pool_copy(g):
        return (
            remote(
                psend.at[g, 1], precv.at[g, 0], pool_send.at[g, 0], pool_recv.at[g, 0], right
            ),
            remote(psend.at[g, 0], precv.at[g, 1], pool_send.at[g, 1], pool_recv.at[g, 1], left),
        )

    def count_copy():
        return (
            remote(counts.at[2], counts.at[3], count_send.at[0], count_recv.at[0], right),
            remote(counts.at[0], counts.at[4], count_send.at[1], count_recv.at[1], left),
        )

    def back_copy(t):
        return (
            remote(back.at[t, 1], back.at[t, 0], back_send.at[t, 0], back_recv.at[t, 0], right),
            remote(back.at[t, 1], back.at[t, 2], back_send.at[t, 1], back_recv.at[t, 1], left),
        )

    def run_pair(first, finish):
        def step(g, c):
            attend(first, g)
            project(first + 1, g)
            send_halo(first + 1, g)
            return c

        lax.fori_loop(0, GROUPS, step, 0)

        def last(g, c):
            finish(g, attend(first + 1, g))
            return c

        lax.fori_loop(0, GROUPS, last, 0)

    late["qkv"].wait()
    project(0, 0)
    pl.semaphore_wait(barrier, n - 1)
    send_halo(0, 0)
    exchange(*count_copy(), True)
    project(0, 1)
    send_halo(0, 1)

    def pair_copy(target, slot):
        return remote(
            pair_hbm.at[(target * per) // samples],
            pair_buf.at[slot],
            pair_send.at[target],
            pair_recv.at[slot],
            target,
        )

    def pair_start(k, c):
        pair_copy(lax.rem(me + k, n), me).start()
        return c

    lax.fori_loop(1, n, pair_start, 0)

    def pool(g, value):
        pooled = jnp.maximum(dot(normed(value).astype(BF16), w_pool_ref[...]), 0.0)
        high = pooled.astype(BF16)
        low = (pooled - high.astype(F32)).astype(BF16)
        for i in range(gs):
            at = slice(i * atom_rows, (i + 1) * atom_rows)
            part = dot(sel, high[at]) + dot(sel, low[at])
            psend[g, 0, i] = part[:token_rows].astype(BF16)
            own_sum[g, i] = part[token_rows : 2 * token_rows]
            psend[g, 1, i] = part[2 * token_rows :].astype(BF16)
        exchange(*pool_copy(g), True)

    late["bias"].wait()
    place = lax.broadcasted_iota(jnp.int32, (1, KEY_WINDOW), 1)
    for b in range(blocks):
        position = me * atom_rows - RIM + QUERY_BLOCK * b + place
        allowed = (position >= edges_ref[0, b]) & (position < edges_ref[1, b])
        masked_bias[b] = jnp.where(
            allowed, bias_ref[b].reshape(atom_heads * QUERY_BLOCK, KEY_WINDOW), -1e30
        )

    @pl.when(jnp.logical_not(has_left))
    def _():
        for layer in range(LAYERS):
            for g in range(GROUPS):
                kv[layer, g, :, 0:RIM, :] = jnp.zeros((gs, RIM, 2 * width), BF16)
        for g in range(GROUPS):
            precv[g, 0] = jnp.zeros(precv.shape[2:], BF16)
        for t in range(waves):
            back[t, 0] = jnp.zeros(back.shape[2:], BF16)
        counts[3] = jnp.zeros(counts.shape[1:], BF16)

    @pl.when(jnp.logical_not(has_right))
    def _():
        for layer in range(LAYERS):
            for g in range(GROUPS):
                kv[layer, g, :, RIM + atom_rows :, :] = jnp.zeros((gs, RIM, 2 * width), BF16)
        for g in range(GROUPS):
            precv[g, 1] = jnp.zeros(precv.shape[2:], BF16)
        for t in range(waves):
            back[t, 2] = jnp.zeros(back.shape[2:], BF16)
        counts[4] = jnp.zeros(counts.shape[1:], BF16)

    for name in ("out", "up", "down", "pool"):
        late[name].wait()
    run_pair(0, pool)
    late["single"].wait()
    late["back"].wait()

    exchange(*count_copy(), False)
    number_of = (
        counts[1].astype(F32)[:, :1] + counts[3].astype(F32)[:, :1] + counts[4].astype(F32)[:, :1]
    )
    lanes = 128
    half = lanes // 2
    lane = lax.broadcasted_iota(jnp.int32, (token_rows, lanes), 1)

    def moved(block, start, to):
        tile, off = start // lanes, start % lanes
        shift = (to - off) % lanes

        def turned(t):
            part = block[:, t * lanes : (t + 1) * lanes]
            return part if shift == 0 else pltpu.roll(part, shift, 1)

        if off + head_size <= lanes:
            return turned(tile)
        return jnp.where(lane < to + lanes - off, turned(tile), turned(tile + 1))

    def spread(copy_of, begin):
        def step(k, c):
            other = lax.rem(me + k, n)
            if begin:
                copy_of(other, me).start()
            else:
                copy = copy_of(other, other)
                copy.wait_send()
                copy.wait_recv()
            return c

        lax.fori_loop(1, n, step, 0)

    def item_copy(t):
        return lambda target, slot: remote(
            items.at[t, target],
            got.at[t, slot],
            item_send.at[t, target],
            item_recv.at[t, slot],
            target,
        )

    def out_copy(t):
        return lambda target, slot: remote(
            outs.at[t, target],
            returned.at[t, slot],
            out_send.at[t, target],
            out_recv.at[t, slot],
            target,
        )

    def token_project(t):
        for g in range(GROUPS) if waves == 1 else (t,):
            exchange(*pool_copy(g), False)
        for a in range(wave_samples):
            s = t * wave_samples + a
            g, i = s // gs, s % gs
            sums = own_sum[g, i] + precv[g, 0, i].astype(F32) + precv[g, 1, i].astype(F32)
            token_in[s * token_rows : (s + 1) * token_rows, :] = (
                sums / number_of + token_single_ref[...]
            )
        normal_tok = normed(token_in[t * wave_rows : (t + 1) * wave_rows, :]).astype(BF16)
        parts = [
            dot(normal_tok, w_tqkv[:, j * channels : (j + 1) * channels]) for j in range(3)
        ]
        for h in range(heads):
            start = h * head_size
            for a in range(0, wave_samples, pack):
                keys = []
                for p in range(pack):
                    item = h * samples + t * wave_samples + a + p
                    owner, unit = item // per, item % per // pack - t * units
                    at = slice((a + p) * token_rows, (a + p + 1) * token_rows)
                    v = moved(parts[2][at], start, half * p)
                    q = moved(parts[0][at], start, half * (1 - p))
                    keys.append(moved(parts[1][at], start, half * (1 - p)))
                    low, high = (v, q) if p == 0 else (q, v)
                    tile = jnp.where(lane < head_size, low, jnp.where(lane < half, 1.0, high))
                    items[t, owner, unit, p * token_rows : (p + 1) * token_rows, :] = tile.astype(
                        BF16
                    )
                key = keys[0] if pack == 1 else jnp.where(lane < half, keys[1], keys[0])
                items[t, owner, unit, pack * token_rows :, :] = key.astype(BF16)
        spread(item_copy(t), True)
        got[t, me] = items[t, me]

    token_scale = head_size ** (-0.5)
    tile = 16
    key_lane = lax.broadcasted_iota(jnp.int32, (tokens, lanes), 1)
    out_lane = lax.broadcasted_iota(jnp.int32, (tile * token_rows, lanes), 1)

    def token_attend(t):
        spread(item_copy(t), False)
        for unit in range(units):
            packed = got[t, :, unit, pack * token_rows :, :].reshape(tokens, lanes)

            def one(block, c):
                span = pl.ds(block * tile, tile)
                ratios = []
                for p in range(pack):
                    at = slice(p * token_rows, (p + 1) * token_rows)
                    mine = key_lane < head_size
                    if p == 0:
                        mine = (key_lane >= half) & (key_lane < half + head_size)
                    keys = jnp.where(mine, packed, jnp.zeros_like(packed))
                    values = got[t, :, unit, at, :].reshape(tokens, lanes)
                    q = got[t, span, unit, at, :].reshape(tile * token_rows, lanes)
                    scores = lax.dot_general(q, keys, LAST, preferred_element_type=F32)
                    scores = scores * token_scale + pair_buf[span].reshape(
                        tile * token_rows, tokens
                    )
                    expo = jnp.exp(scores - jnp.max(scores, -1, keepdims=True)).astype(BF16)
                    both = dot(expo, values)
                    ratios.append(both / both[:, head_size : head_size + 1])
                ratio = ratios[0] if pack == 1 else jnp.where(out_lane < half, *ratios)
                outs[t, span, unit, :, :] = ratio.astype(BF16).reshape(tile, token_rows, lanes)
                return c

            if n == tile:
                one(0, 0)
            else:
                lax.fori_loop(0, n // tile, one, 0)
        spread(out_copy(t), True)
        returned[t, me] = outs[t, me]

    def token_finish(t):
        spread(out_copy(t), False)
        state = token_in[t * wave_rows : (t + 1) * wave_rows, :]
        for h in range(heads):
            mix = []
            for a in range(wave_samples):
                item = h * samples + t * wave_samples + a
                owner, unit, p = item // per, item % per // pack - t * units, item % per % pack
                block = returned[t, owner, unit]
                if p == 1:
                    block = pltpu.roll(block.astype(F32), half, 1).astype(BF16)
                mix.append(block[:, :head_size])
            state = state + dot(
                jnp.concatenate(mix, axis=0), w_tout[h * head_size : (h + 1) * head_size, :]
            )
        for a in range(wave_samples):
            state_ref[t * wave_samples + a] = state[a * token_rows : (a + 1) * token_rows]
        back[t, 1] = dot(normed(state).astype(BF16), w_back_ref[...]).astype(BF16)
        exchange(*back_copy(t), True)

    load_tqkv.wait()
    for t in range(waves):
        token_project(t)
    own_pair.wait()
    spread(pair_copy, False)
    for t in range(waves):
        token_attend(t)
    load_tout.wait()
    for t in range(waves):
        token_finish(t)
    first = ENC_LAYERS
    for g in range(GROUPS):
        for t in range(waves):
            if g * waves // GROUPS == t and (waves == GROUPS or g == 0):
                exchange(*back_copy(t), False)
        for i in range(gs):
            s = g * gs + i
            t, at = s // wave_samples, s % wave_samples * token_rows
            near = jnp.concatenate([back[t, j, at : at + token_rows, :] for j in range(3)], axis=0)
            picked = lax.dot_general(sel, near, FIRST, preferred_element_type=F32)
            stream[g, i * atom_rows : (i + 1) * atom_rows, :] += picked
        project(first, g)
        send_halo(first, g)

    def finish(g, value):
        normal = normed(value).astype(BF16)
        for i in range(gs):
            s = g * gs + i
            update = lax.dot_general(
                w_final_ref[...],
                normal[i * atom_rows : (i + 1) * atom_rows],
                LAST,
                preferred_element_type=F32,
            )
            sigma, total = sigma_of(s)
            result = (
                SIGMA_DATA * SIGMA_DATA / total * noisy_of(s, sigma)
                + sigma * SIGMA_DATA * lax.rsqrt(total) * update
            ) / SIGMA_DATA
            for c in range(3):
                denoised_ref[c, pl.ds(s, 1), :] = result[c : c + 1]

    run_pair(first, finish)


def shards(
    n,
    x_true,
    noise,
    noise_level,
    atom_single,
    atom_token,
    window_edges,
    atom_pair_bias,
    token_single,
    pair_bias,
    w_coord,
    w_atom_qkv,
    w_atom_out,
    w_atom_up,
    w_atom_down,
    w_pool,
    w_token_qkv,
    w_token_out,
    w_back,
    w_final,
):
    samples = noise.shape[0]
    atom_rows, width = atom_single.shape
    token_rows, channels = token_single.shape
    blocks, atom_heads = atom_pair_bias.shape[:2]
    heads = pair_bias.shape[0]
    gs = samples // GROUPS
    per, pack, waves, units = plan(n, heads, samples)
    vmem = pl.BlockSpec(memory_space=pltpu.VMEM)
    smem = pl.BlockSpec(memory_space=pltpu.SMEM)
    anywhere = pl.BlockSpec(memory_space=pl.ANY)
    dma = pltpu.SemaphoreType.DMA
    denoised, state = pl.pallas_call(
        functools.partial(kernel, n),
        name="denoise",
        out_shape=(
            jax.ShapeDtypeStruct((3, samples, atom_rows), F32),
            jax.ShapeDtypeStruct((samples, token_rows, channels), F32),
        ),
        in_specs=[smem, smem]
        + [vmem] * 4
        + [anywhere] * 3
        + [vmem]
        + [anywhere] * 8
        + [vmem],
        out_specs=(vmem, vmem),
        scratch_shapes=[
            pltpu.VMEM((GROUPS, gs * atom_rows, width), F32),
            pltpu.VMEM((LAYERS, GROUPS, gs, atom_rows + 2 * RIM, 2 * width), BF16),
            pltpu.VMEM((GROUPS, gs * atom_rows, width), BF16),
            pltpu.VMEM((blocks, atom_heads * QUERY_BLOCK, KEY_WINDOW), F32),
            pltpu.VMEM((5, token_rows, 128), BF16),
            pltpu.VMEM((GROUPS, gs, token_rows, channels), F32),
            pltpu.VMEM((GROUPS, 2, gs, token_rows, channels), BF16),
            pltpu.VMEM((GROUPS, 2, gs, token_rows, channels), BF16),
            pltpu.VMEM((samples * token_rows, channels), F32),
            pltpu.VMEM((waves, n, units, (pack + 1) * token_rows, 128), BF16),
            pltpu.VMEM((waves, n, units, (pack + 1) * token_rows, 128), BF16),
            pltpu.VMEM((n, token_rows, n * token_rows), F32),
            pltpu.VMEM((waves, n, units, token_rows, 128), BF16),
            pltpu.VMEM((waves, n, units, token_rows, 128), BF16),
            pltpu.VMEM((waves, 3, samples // waves * token_rows, width), BF16),
            pltpu.VMEM(w_token_qkv.shape, BF16),
            pltpu.VMEM(w_token_out.shape, BF16),
            pltpu.VMEM(atom_pair_bias.shape, F32),
            pltpu.VMEM(token_single.shape, F32),
            pltpu.VMEM(w_atom_qkv.shape, BF16),
            pltpu.VMEM(w_atom_out.shape, BF16),
            pltpu.VMEM(w_atom_up.shape, BF16),
            pltpu.VMEM(w_atom_down.shape, BF16),
            pltpu.VMEM(w_pool.shape, BF16),
            pltpu.VMEM(w_back.shape, BF16),
            dma((3,)),
            dma((8,)),
            dma((LAYERS, GROUPS, 2)),
            dma((LAYERS, GROUPS, 2)),
            dma((2,)),
            dma((2,)),
            dma((GROUPS, 2)),
            dma((GROUPS, 2)),
            dma((n,)),
            dma((n,)),
            dma((waves, n)),
            dma((waves, n)),
            dma((waves, n)),
            dma((waves, n)),
            dma((waves, 2)),
            dma((waves, 2)),
        ],
        compiler_params=pltpu.CompilerParams(
            collective_id=0, has_side_effects=True, vmem_limit_bytes=56 * 1024 * 1024
        ),
    )(
        noise_level,
        window_edges.T,
        x_true,
        noise.transpose(1, 0, 2),
        atom_single,
        atom_token.reshape(1, atom_rows),
        atom_pair_bias,
        token_single,
        pair_bias,
        w_coord,
        w_atom_qkv,
        w_atom_out,
        w_atom_up,
        w_atom_down,
        w_pool,
        w_token_qkv,
        w_token_out,
        w_back,
        w_final,
    )
    return denoised.transpose(1, 0, 2), state


def solution(mesh):
    in_specs = (
        P(None, ("groups", "seq")),
        P("groups", None, "seq"),
        P("groups"),
        P(("groups", "seq"), None),
        P(("groups", "seq")),
        P(("groups", "seq"), None),
        P(("groups", "seq"), None, None, None),
        P(("groups", "seq"), None),
        P("groups", "seq", None),
    ) + (P(),) * 10
    out_specs = (P("groups", None, "seq"), P("groups", "seq", None))
    return jax.shard_map(
        functools.partial(shards, mesh.shape["seq"]),
        mesh=mesh,
        in_specs=in_specs,
        out_specs=out_specs,
        check_vma=False,
    )
```

profile of v0, /device:TPU:1, one launch (start us, length us, event | category | flops | bytes accessed | tf_op | source)
XLA Modules:
  0.0 54.2 jit_solution(17143480933438610095)
XLA Ops:
  0.6 50.7 %denoise.1 = (f32[3,4,128]{2,1,0:T(4,128)}, f32[4,16,768]{2,1,0:T(8,128)}) custom-call(s32[4]{0:T(128)} %level_ref.1, s32[2,4]{1,0:T(2,128)} %bitcast.6, f32[3,128]{1,0:T(4,128)} %x_true_ref.1, f32[3,4,128]{2,1,0:T(4,128)} %bitcast.4, bf16[128,128]{1,0:T(8,128)(2,1)} %single_ref.1, s32[1,128]{1,0:T(1,128)} %bitcast.7, f32[4,4,32,128]{3,2,1,0:T(8,128)} %bias_hbm.1, ...), custom_call_target="tpu_custom_call" | custom-call | tf_op jit(solution)/shard_map/denoise/pallas_call | solution.py:640
  51.3 1.3 %copy.23 = f32[4,3,128]{2,0,1:T(4,128)} copy(f32[4,3,128]{2,0,1:T(4,128)} %bitcast.5) | data formatting | bytes 12288
  52.6 1.6 %copy.24 = f32[4,16,768]{2,1,0:T(8,128)} copy(f32[4,16,768]{2,1,0:T(8,128)} %get-tuple-element.9) | data formatting | bytes 393216
where the time goes:
time: 54.7 us; the launch traced here: 54.2 us
  Pallas kernels  50.7 us (93%)
  local copies, waits for them, and re-layouts  2.9 us (5%)
  between operations  0.65 us (1%)
    pallas_call x1, Pallas kernels, shards(): pl.pallas_call(functools.partial(kernel, n), name='denoise', out_shape=(j...  50.7 us
    unnamed x2, local copies, waits for them, and re-layouts  2.9 us

commit v1 on v0

--- a/solution.py
+++ b/solution.py
@@ -604,6 +604,17 @@
     run_pair(first, finish)
 
 
+def store(denoised_ref, state_ref, denoised_out, state_out, sem):
+    copies = (
+        pltpu.make_async_copy(state_ref, state_out, sem.at[0]),
+        pltpu.make_async_copy(denoised_ref, denoised_out, sem.at[1]),
+    )
+    for copy in copies:
+        copy.start()
+    for copy in copies:
+        copy.wait()
+
+
 def shards(
     n,
     x_true,
@@ -637,12 +648,12 @@
     smem = pl.BlockSpec(memory_space=pltpu.SMEM)
     anywhere = pl.BlockSpec(memory_space=pl.ANY)
     dma = pltpu.SemaphoreType.DMA
-    denoised, state = pl.pallas_call(
+    held = pl.pallas_call(
         functools.partial(kernel, n),
         name="denoise",
         out_shape=(
-            jax.ShapeDtypeStruct((3, samples, atom_rows), F32),
-            jax.ShapeDtypeStruct((samples, token_rows, channels), F32),
+            pltpu.VMEM((3, samples, atom_rows), F32),
+            pltpu.VMEM((samples, token_rows, channels), F32),
         ),
         in_specs=[smem, smem]
         + [vmem] * 4
@@ -718,6 +729,17 @@
         w_back,
         w_final,
     )
+    denoised, state = pl.pallas_call(
+        store,
+        name="store",
+        out_shape=(
+            jax.ShapeDtypeStruct((3, samples, atom_rows), F32),
+            jax.ShapeDtypeStruct((samples, token_rows, channels), F32),
+        ),
+        in_specs=[vmem] * 2,
+        out_specs=(anywhere, anywhere),
+        scratch_shapes=[dma((2,))],
+    )(*[pltpu.with_memory_space_constraint(x, pltpu.VMEM) for x in held])
     return denoised.transpose(1, 0, 2), state
 
 

time: 54.7 us -> 51.8 us (0.947)
  local copies, waits for them, and re-layouts: 2.9 us -> 0 us
    unnamed x2 -> x0, local copies, waits for them, and re-layouts: 2.9 us -> none
    pallas_call x1 -> x2, Pallas kernels: 50.7 us -> 50.8 us  [the longest x1 50.1 us: shards(): pl.pallas_call(functools.partial(kernel, n), name='denoise', out_shape=(p...]
where the time goes in v1:
time: 51.8 us; the launch traced here: 51.4 us
  Pallas kernels  50.8 us (98%)
  between operations  0.65 us (1%)
    pallas_call x1, Pallas kernels, shards(): pl.pallas_call(functools.partial(kernel, n), name='denoise', out_shape=(p...  50.1 us

profile of v1, /device:TPU:1, one launch (start us, length us, event | category | flops | bytes accessed | tf_op | source)
XLA Modules:
  0.0 51.4 jit_solution(5820515213860520900)
XLA Ops:
  0.6 50.1 %denoise.1 = (f32[3,4,128]{2,1,0:T(4,128)S(1)}, f32[4,16,768]{2,1,0:T(8,128)S(1)}) custom-call(s32[4]{0:T(128)} %level_ref.1, s32[2,4]{1,0:T(2,128)} %bitcast.5, f32[3,128]{1,0:T(4,128)} %x_true_ref.1, f32[3,4,128]{2,1,0:T(4,128)} %bitcast.4, bf16[128,128]{1,0:T(8,128)(2,1)} %single_ref.1, s32[1,128]{1,0:T(1,128)} %bitcast.6, f32[4,4,32,128]{3,2,1,0:T(8,128)} %bias_hbm.1, ...), custom_call_target="tpu_custom_call" | custom-call | tf_op jit(solution)/shard_map/denoise/pallas_call | solution.py:651
  50.7 0.7 %store.1 = (f32[3,4,128]{2,1,0:T(4,128)}, f32[4,16,768]{2,1,0:T(8,128)}) custom-call(f32[3,4,128]{2,1,0:T(4,128)S(1)} %get-tuple-element.6.denoised_ref, f32[4,16,768]{2,1,0:T(8,128)S(1)} %get-tuple-element.7.state_ref), custom_call_target="tpu_custom_call" | custom-call | tf_op jit(solution)/shard_map/store/pallas_call | solution.py:732

commit v2 on v1

--- a/solution.py
+++ b/solution.py
@@ -55,16 +55,16 @@
 
 def kernel(
     n,
-    level_ref,
-    edges_ref,
-    x_true_ref,
-    noise_ref,
-    single_ref,
-    atom_token_ref,
+    level_hbm,
+    edges_hbm,
+    x_true_hbm,
+    noise_hbm,
+    single_hbm,
+    atom_token_hbm,
     bias_hbm,
     token_single_hbm,
     pair_hbm,
-    w_coord_ref,
+    w_coord_hbm,
     w_qkv_hbm,
     w_out_hbm,
     w_up_hbm,
@@ -73,9 +73,17 @@
     w_tqkv_hbm,
     w_tout_hbm,
     w_back_hbm,
-    w_final_ref,
+    w_final_hbm,
     denoised_ref,
     state_ref,
+    level_ref,
+    edges_ref,
+    x_true_ref,
+    noise_ref,
+    single_ref,
+    atom_token_ref,
+    w_coord_ref,
+    w_final_ref,
     stream,
     kv,
     queries,
@@ -101,8 +109,7 @@
     w_down_ref,
     w_pool_ref,
     w_back_ref,
-    w_sem,
-    late_sem,
+    load_sem,
     halo_send,
     halo_recv,
     count_send,
@@ -145,29 +152,35 @@
         )
         return c
 
-    lax.fori_loop(1, n, greet, 0)
-    load_tqkv = pltpu.make_async_copy(w_tqkv_hbm, w_tqkv, w_sem.at[0])
-    load_tout = pltpu.make_async_copy(w_tout_hbm, w_tout, w_sem.at[1])
-    late = {}
+    own_head = (me * per) // samples
+    loads = {}
     for slot, (name, src, dst) in enumerate(
         (
+            ("level", level_hbm, level_ref),
+            ("x_true", x_true_hbm, x_true_ref),
+            ("noise", noise_hbm, noise_ref),
+            ("atoms", single_hbm, single_ref),
+            ("coord", w_coord_hbm, w_coord_ref),
             ("qkv", w_qkv_hbm, w_qkv_ref),
+            ("atom_token", atom_token_hbm, atom_token_ref),
+            ("edges", edges_hbm, edges_ref),
             ("bias", bias_hbm, bias_ref),
             ("out", w_out_hbm, w_out_ref),
             ("up", w_up_hbm, w_up_ref),
             ("down", w_down_hbm, w_down_ref),
             ("pool", w_pool_hbm, w_pool_ref),
             ("single", token_single_hbm, token_single_ref),
+            ("tqkv", w_tqkv_hbm, w_tqkv),
             ("back", w_back_hbm, w_back_ref),
+            ("tout", w_tout_hbm, w_tout),
+            ("final", w_final_hbm, w_final_ref),
+            ("own_pair", pair_hbm.at[own_head], pair_buf.at[me]),
         )
     ):
-        late[name] = pltpu.make_async_copy(src, dst, late_sem.at[slot])
-        late[name].start()
-    load_tqkv.start()
-    load_tout.start()
-    own_head = (me * per) // samples
-    own_pair = pltpu.make_async_copy(pair_hbm.at[own_head], pair_buf.at[me], w_sem.at[2])
-    own_pair.start()
+        loads[name] = pltpu.make_async_copy(src, dst, load_sem.at[slot])
+        loads[name].start()
+        if name == "qkv":
+            lax.fori_loop(1, n, greet, 0)
 
     upper_root = 160.0 ** (1.0 / 7.0)
     lower_root = 0.0004 ** (1.0 / 7.0)
@@ -183,6 +196,8 @@
         noise = jnp.concatenate([noise_ref[c, pl.ds(s, 1), :] for c in range(3)], axis=0)
         return x_true_ref[...] + sigma * noise
 
+    for name in ("level", "x_true", "noise"):
+        loads[name].wait()
     scaled = []
     for s in range(samples):
         sigma, total = sigma_of(s)
@@ -191,6 +206,8 @@
     columns = jnp.transpose(
         jnp.concatenate(scaled + [jnp.zeros((spare, atom_rows), F32)], axis=0)
     )
+    loads["atoms"].wait()
+    loads["coord"].wait()
     single = single_ref[...].astype(F32)
     for s in range(samples):
         value = single
@@ -199,15 +216,6 @@
             value = value + columns[:, at : at + 1] * w_coord_ref[c : c + 1, :]
         stream[s // gs, pl.ds((s % gs) * atom_rows, atom_rows), :] = value
 
-    relative = atom_token_ref[...] - (me - 1) * token_rows
-    selector = (
-        lax.broadcasted_iota(jnp.int32, (3 * token_rows, atom_rows), 0) == relative
-    ).astype(F32)
-    sel = selector.astype(BF16)
-    counted = jnp.broadcast_to(jnp.sum(selector, 1, keepdims=True), (3 * token_rows, 128))
-    for j in range(3):
-        counts[j] = counted[j * token_rows : (j + 1) * token_rows].astype(BF16)
-
     def exchange(to_right, to_left, begin):
         if begin:
 
@@ -224,26 +232,33 @@
             @pl.when(has_left)
             def _():
                 to_right.wait_recv()
-                to_left.wait_send()
 
             @pl.when(has_right)
             def _():
                 to_left.wait_recv()
-                to_right.wait_send()
+
+    def sent(to_right, to_left):
+        @pl.when(has_right)
+        def _():
+            to_right.wait_send()
+
+        @pl.when(has_left)
+        def _():
+            to_left.wait_send()
 
     def halo(layer, g):
         return (
             remote(
                 kv.at[layer, g, :, pl.ds(atom_rows, RIM), :],
                 kv.at[layer, g, :, pl.ds(0, RIM), :],
-                halo_send.at[layer, g, 0],
+                halo_send.at[0],
                 halo_recv.at[layer, g, 0],
                 right,
             ),
             remote(
                 kv.at[layer, g, :, pl.ds(RIM, RIM), :],
                 kv.at[layer, g, :, pl.ds(RIM + atom_rows, RIM), :],
-                halo_send.at[layer, g, 1],
+                halo_send.at[1],
                 halo_recv.at[layer, g, 1],
                 left,
             ),
@@ -310,9 +325,9 @@
     def pool_copy(g):
         return (
             remote(
-                psend.at[g, 1], precv.at[g, 0], pool_send.at[g, 0], pool_recv.at[g, 0], right
+                psend.at[g, 1], precv.at[g, 0], pool_send.at[0], pool_recv.at[g, 0], right
             ),
-            remote(psend.at[g, 0], precv.at[g, 1], pool_send.at[g, 1], pool_recv.at[g, 1], left),
+            remote(psend.at[g, 0], precv.at[g, 1], pool_send.at[1], pool_recv.at[g, 1], left),
         )
 
     def count_copy():
@@ -323,8 +338,8 @@
 
     def back_copy(t):
         return (
-            remote(back.at[t, 1], back.at[t, 0], back_send.at[t, 0], back_recv.at[t, 0], right),
-            remote(back.at[t, 1], back.at[t, 2], back_send.at[t, 1], back_recv.at[t, 1], left),
+            remote(back.at[t, 1], back.at[t, 0], back_send.at[0], back_recv.at[t, 0], right),
+            remote(back.at[t, 1], back.at[t, 2], back_send.at[1], back_recv.at[t, 1], left),
         )
 
     def run_pair(first, finish):
@@ -342,20 +357,30 @@
 
         lax.fori_loop(0, GROUPS, last, 0)
 
-    late["qkv"].wait()
+    loads["qkv"].wait()
     project(0, 0)
     pl.semaphore_wait(barrier, n - 1)
     send_halo(0, 0)
-    exchange(*count_copy(), True)
     project(0, 1)
     send_halo(0, 1)
+    loads["atom_token"].wait()
+    relative = atom_token_ref[...] - (me - 1) * token_rows
+    selector = (
+        lax.broadcasted_iota(jnp.int32, (3 * token_rows, atom_rows), 0) == relative
+    ).astype(F32)
+    sel = selector.astype(BF16)
+    counted = jnp.broadcast_to(jnp.sum(selector, 1, keepdims=True), (3 * token_rows, 128))
+    for j in range(3):
+        counts[j] = counted[j * token_rows : (j + 1) * token_rows].astype(BF16)
+
+    exchange(*count_copy(), True)
 
     def pair_copy(target, slot):
         return remote(
             pair_hbm.at[(target * per) // samples],
             pair_buf.at[slot],
-            pair_send.at[target],
-            pair_recv.at[slot],
+            pair_send,
+            pair_recv,
             target,
         )
 
@@ -377,7 +402,8 @@
             psend[g, 1, i] = part[2 * token_rows :].astype(BF16)
         exchange(*pool_copy(g), True)
 
-    late["bias"].wait()
+    loads["bias"].wait()
+    loads["edges"].wait()
     place = lax.broadcasted_iota(jnp.int32, (1, KEY_WINDOW), 1)
     for b in range(blocks):
         position = me * atom_rows - RIM + QUERY_BLOCK * b + place
@@ -409,10 +435,10 @@
         counts[4] = jnp.zeros(counts.shape[1:], BF16)
 
     for name in ("out", "up", "down", "pool"):
-        late[name].wait()
+        loads[name].wait()
     run_pair(0, pool)
-    late["single"].wait()
-    late["back"].wait()
+    loads["single"].wait()
+    loads["back"].wait()
 
     exchange(*count_copy(), False)
     number_of = (
@@ -434,35 +460,38 @@
             return turned(tile)
         return jnp.where(lane < to + lanes - off, turned(tile), turned(tile + 1))
 
-    def spread(copy_of, begin):
+    def spread(copy_of):
         def step(k, c):
-            other = lax.rem(me + k, n)
-            if begin:
-                copy_of(other, me).start()
-            else:
-                copy = copy_of(other, other)
-                copy.wait_send()
-                copy.wait_recv()
+            copy_of(lax.rem(me + k, n), me).start()
             return c
 
         lax.fori_loop(1, n, step, 0)
+
+    others = pl.ds(0, n - 1)
+
+    def every_pair():
+        return remote(
+            pair_buf.at[others], pair_buf.at[others], pair_send, pair_recv, right
+        )
 
     def item_copy(t):
         return lambda target, slot: remote(
-            items.at[t, target],
-            got.at[t, slot],
-            item_send.at[t, target],
-            item_recv.at[t, slot],
-            target,
+            items.at[t, target], got.at[t, slot], item_send, item_recv.at[t], target
+        )
+
+    def every_item(t):
+        return remote(
+            items.at[t, others], got.at[t, others], item_send, item_recv.at[t], right
         )
 
     def out_copy(t):
         return lambda target, slot: remote(
-            outs.at[t, target],
-            returned.at[t, slot],
-            out_send.at[t, target],
-            out_recv.at[t, slot],
-            target,
+            outs.at[t, target], returned.at[t, slot], out_send, out_recv.at[t], target
+        )
+
+    def every_out(t):
+        return remote(
+            outs.at[t, others], returned.at[t, others], out_send, out_recv.at[t], right
         )
 
     def token_project(t):
@@ -497,7 +526,7 @@
                     )
                 key = keys[0] if pack == 1 else jnp.where(lane < half, keys[1], keys[0])
                 items[t, owner, unit, pack * token_rows :, :] = key.astype(BF16)
-        spread(item_copy(t), True)
+        spread(item_copy(t))
         got[t, me] = items[t, me]
 
     token_scale = head_size ** (-0.5)
@@ -506,7 +535,7 @@
     out_lane = lax.broadcasted_iota(jnp.int32, (tile * token_rows, lanes), 1)
 
     def token_attend(t):
-        spread(item_copy(t), False)
+        every_item(t).wait_recv()
         for unit in range(units):
             packed = got[t, :, unit, pack * token_rows :, :].reshape(tokens, lanes)
 
@@ -536,11 +565,11 @@
                 one(0, 0)
             else:
                 lax.fori_loop(0, n // tile, one, 0)
-        spread(out_copy(t), True)
+        spread(out_copy(t))
         returned[t, me] = outs[t, me]
 
     def token_finish(t):
-        spread(out_copy(t), False)
+        every_out(t).wait_recv()
         state = token_in[t * wave_rows : (t + 1) * wave_rows, :]
         for h in range(heads):
             mix = []
@@ -559,14 +588,14 @@
         back[t, 1] = dot(normed(state).astype(BF16), w_back_ref[...]).astype(BF16)
         exchange(*back_copy(t), True)
 
-    load_tqkv.wait()
+    loads["tqkv"].wait()
     for t in range(waves):
         token_project(t)
-    own_pair.wait()
-    spread(pair_copy, False)
+    loads["own_pair"].wait()
+    every_pair().wait_recv()
     for t in range(waves):
         token_attend(t)
-    load_tout.wait()
+    loads["tout"].wait()
     for t in range(waves):
         token_finish(t)
     first = ENC_LAYERS
@@ -601,7 +630,38 @@
             for c in range(3):
                 denoised_ref[c, pl.ds(s, 1), :] = result[c : c + 1]
 
+    loads["final"].wait()
     run_pair(first, finish)
+
+    sent(
+        remote(
+            kv.at[:, :, :, pl.ds(0, RIM), :],
+            kv.at[:, :, :, pl.ds(0, RIM), :],
+            halo_send.at[0],
+            halo_recv.at[0, 0, 0],
+            right,
+        ),
+        remote(
+            kv.at[:, :, :, pl.ds(0, RIM), :],
+            kv.at[:, :, :, pl.ds(0, RIM), :],
+            halo_send.at[1],
+            halo_recv.at[0, 0, 1],
+            left,
+        ),
+    )
+    sent(*count_copy())
+    sent(
+        remote(psend.at[:, 1], precv.at[:, 0], pool_send.at[0], pool_recv.at[0, 0], right),
+        remote(psend.at[:, 0], precv.at[:, 1], pool_send.at[1], pool_recv.at[0, 1], left),
+    )
+    sent(
+        remote(back.at[:, 1], back.at[:, 0], back_send.at[0], back_recv.at[0, 0], right),
+        remote(back.at[:, 1], back.at[:, 2], back_send.at[1], back_recv.at[0, 1], left),
+    )
+    every_pair().wait_send()
+    for t in range(waves):
+        every_item(t).wait_send()
+        every_out(t).wait_send()
 
 
 def store(denoised_ref, state_ref, denoised_out, state_out, sem):
@@ -645,7 +705,6 @@
     gs = samples // GROUPS
     per, pack, waves, units = plan(n, heads, samples)
     vmem = pl.BlockSpec(memory_space=pltpu.VMEM)
-    smem = pl.BlockSpec(memory_space=pltpu.SMEM)
     anywhere = pl.BlockSpec(memory_space=pl.ANY)
     dma = pltpu.SemaphoreType.DMA
     held = pl.pallas_call(
@@ -655,14 +714,17 @@
             pltpu.VMEM((3, samples, atom_rows), F32),
             pltpu.VMEM((samples, token_rows, channels), F32),
         ),
-        in_specs=[smem, smem]
-        + [vmem] * 4
-        + [anywhere] * 3
-        + [vmem]
-        + [anywhere] * 8
-        + [vmem],
+        in_specs=[anywhere] * 19,
         out_specs=(vmem, vmem),
         scratch_shapes=[
+            pltpu.SMEM((samples,), jnp.int32),
+            pltpu.SMEM((2, blocks), jnp.int32),
+            pltpu.VMEM(x_true.shape, F32),
+            pltpu.VMEM((3, samples, atom_rows), F32),
+            pltpu.VMEM(atom_single.shape, BF16),
+            pltpu.VMEM((1, atom_rows), jnp.int32),
+            pltpu.VMEM(w_coord.shape, F32),
+            pltpu.VMEM(w_final.shape, BF16),
             pltpu.VMEM((GROUPS, gs * atom_rows, width), F32),
             pltpu.VMEM((LAYERS, GROUPS, gs, atom_rows + 2 * RIM, 2 * width), BF16),
             pltpu.VMEM((GROUPS, gs * atom_rows, width), BF16),
@@ -688,21 +750,20 @@
             pltpu.VMEM(w_atom_down.shape, BF16),
             pltpu.VMEM(w_pool.shape, BF16),
             pltpu.VMEM(w_back.shape, BF16),
-            dma((3,)),
-            dma((8,)),
-            dma((LAYERS, GROUPS, 2)),
+            dma((19,)),
+            dma((2,)),
             dma((LAYERS, GROUPS, 2)),
             dma((2,)),
             dma((2,)),
+            dma((2,)),
             dma((GROUPS, 2)),
-            dma((GROUPS, 2)),
-            dma((n,)),
-            dma((n,)),
-            dma((waves, n)),
-            dma((waves, n)),
-            dma((waves, n)),
-            dma((waves, n)),
-            dma((waves, 2)),
+            dma(()),
+            dma(()),
+            dma(()),
+            dma((waves,)),
+            dma(()),
+            dma((waves,)),
+            dma((2,)),
             dma((waves, 2)),
         ],
         compiler_params=pltpu.CompilerParams(

time: 51.8 us -> 49.5 us (0.956)
  Pallas kernels: 50.8 us -> 48.6 us
    pallas_call x1, Pallas kernels: 50.1 us -> 47.9 us  [shards(): pl.pallas_call(functools.partial(kernel, n), name='denoise', out_shape=(p...]
where the time goes in v2:
time: 49.5 us; the launch traced here: 49.2 us
  Pallas kernels  48.6 us (98%)
  between operations  0.65 us (1%)
    pallas_call x1, Pallas kernels, shards(): pl.pallas_call(functools.partial(kernel, n), name='denoise', out_shape=(p...  47.9 us

profile of v2, /device:TPU:1, one launch (start us, length us, event | category | flops | bytes accessed | tf_op | source)
XLA Modules:
  0.0 49.2 jit_solution(15890282301738167813)
XLA Ops:
  0.6 47.9 %denoise.1 = (f32[3,4,128]{2,1,0:T(4,128)S(1)}, f32[4,16,768]{2,1,0:T(8,128)S(1)}) custom-call(s32[4]{0:T(128)} %level_hbm.1, s32[2,4]{1,0:T(2,128)} %bitcast.5, f32[3,128]{1,0:T(4,128)} %x_true_hbm.1, f32[3,4,128]{2,1,0:T(4,128)} %bitcast.4, bf16[128,128]{1,0:T(8,128)(2,1)} %single_hbm.1, s32[1,128]{1,0:T(1,128)} %bitcast.6, f32[4,4,32,128]{3,2,1,0:T(8,128)} %bias_hbm.1, ...), custom_call_target="tpu_custom_call" | custom-call | tf_op jit(solution)/shard_map/denoise/pallas_call | solution.py:710
  48.5 0.7 %store.1 = (f32[3,4,128]{2,1,0:T(4,128)}, f32[4,16,768]{2,1,0:T(8,128)}) custom-call(f32[3,4,128]{2,1,0:T(4,128)S(1)} %get-tuple-element.6.denoised_ref, f32[4,16,768]{2,1,0:T(8,128)S(1)} %get-tuple-element.7.state_ref), custom_call_target="tpu_custom_call" | custom-call | tf_op jit(solution)/shard_map/store/pallas_call | solution.py:793

commit v3 on v2

--- a/solution.py
+++ b/solution.py
@@ -51,6 +51,12 @@
     pack = 2 if per % 2 == 0 else 1
     waves = GROUPS if per == samples and gs == pack else 1
     return per, pack, waves, per // pack // waves
+
+
+def item_rows(token_rows, pack, waves):
+    if waves == 1:
+        return ((pack + 1) * token_rows,)
+    return 2 * token_rows, 2 * token_rows + token_rows // 2
 
 
 def kernel(
@@ -95,6 +101,8 @@
     token_in,
     items,
     got,
+    held,
+    weights,
     pair_buf,
     outs,
     returned,
@@ -347,12 +355,20 @@
             attend(first, g)
             project(first + 1, g)
             send_halo(first + 1, g)
+            if first == 0:
+                pair_batch(g)
             return c
 
         lax.fori_loop(0, GROUPS, step, 0)
 
         def last(g, c):
             finish(g, attend(first + 1, g))
+            if first == 0:
+
+                @pl.when(g == 0)
+                def _():
+                    pair_batch(2)
+
             return c
 
         lax.fori_loop(0, GROUPS, last, 0)
@@ -388,7 +404,12 @@
         pair_copy(lax.rem(me + k, n), me).start()
         return c
 
-    lax.fori_loop(1, n, pair_start, 0)
+    third = (n - 1) // 3
+
+    def pair_batch(number):
+        low = 1 + number * third
+        high = jnp.where(number == 2, n, low + third)
+        lax.fori_loop(low, high, pair_start, 0)
 
     def pool(g, value):
         pooled = jnp.maximum(dot(normed(value).astype(BF16), w_pool_ref[...]), 0.0)
@@ -446,9 +467,11 @@
     )
     lanes = 128
     half = lanes // 2
+    main = lanes - 2 * head_size
+    rest = head_size - main
     lane = lax.broadcasted_iota(jnp.int32, (token_rows, lanes), 1)
 
-    def moved(block, start, to):
+    def moved(block, start, to, size=head_size):
         tile, off = start // lanes, start % lanes
         shift = (to - off) % lanes
 
@@ -456,7 +479,7 @@
             part = block[:, t * lanes : (t + 1) * lanes]
             return part if shift == 0 else pltpu.roll(part, shift, 1)
 
-        if off + head_size <= lanes:
+        if off + size <= lanes:
             return turned(tile)
         return jnp.where(lane < to + lanes - off, turned(tile), turned(tile + 1))
 
@@ -474,14 +497,19 @@
             pair_buf.at[others], pair_buf.at[others], pair_send, pair_recv, right
         )
 
+    rows_of = item_rows(token_rows, pack, waves)
+    starts = (0, rows_of[0])
+
     def item_copy(t):
+        span = pl.ds(starts[t], rows_of[t])
         return lambda target, slot: remote(
-            items.at[t, target], got.at[t, slot], item_send, item_recv.at[t], target
+            items.at[target, :, span], got.at[slot, :, span], item_send, item_recv.at[t], target
         )
 
     def every_item(t):
+        span = pl.ds(starts[t], rows_of[t])
         return remote(
-            items.at[t, others], got.at[t, others], item_send, item_recv.at[t], right
+            items.at[others, :, span], got.at[others, :, span], item_send, item_recv.at[t], right
         )
 
     def out_copy(t):
@@ -508,26 +536,55 @@
         parts = [
             dot(normal_tok, w_tqkv[:, j * channels : (j + 1) * channels]) for j in range(3)
         ]
-        for h in range(heads):
+        for h in range(heads) if waves == 1 else ():
             start = h * head_size
             for a in range(0, wave_samples, pack):
                 keys = []
                 for p in range(pack):
-                    item = h * samples + t * wave_samples + a + p
-                    owner, unit = item // per, item % per // pack - t * units
+                    item = h * samples + a + p
+                    owner, unit = item // per, item % per // pack
                     at = slice((a + p) * token_rows, (a + p + 1) * token_rows)
                     v = moved(parts[2][at], start, half * p)
                     q = moved(parts[0][at], start, half * (1 - p))
                     keys.append(moved(parts[1][at], start, half * (1 - p)))
                     low, high = (v, q) if p == 0 else (q, v)
                     tile = jnp.where(lane < head_size, low, jnp.where(lane < half, 1.0, high))
-                    items[t, owner, unit, p * token_rows : (p + 1) * token_rows, :] = tile.astype(
+                    items[owner, unit, p * token_rows : (p + 1) * token_rows, :] = tile.astype(
                         BF16
                     )
                 key = keys[0] if pack == 1 else jnp.where(lane < half, keys[1], keys[0])
-                items[t, owner, unit, pack * token_rows :, :] = key.astype(BF16)
+                items[owner, unit, pack * token_rows :, :] = key.astype(BF16)
+        if waves == 2:
+            if t == 0:
+                held[...] = parts[2]
+            one, two = slice(0, token_rows), slice(token_rows, 2 * token_rows)
+            for h in range(heads):
+                start = h * head_size
+                mixed = []
+                for upper, lower, at in ((0, 1, one), (1, 0, two)):
+                    low = moved(parts[upper][one], start, 0)
+                    mid = moved(parts[lower][two], start, head_size)
+                    high = moved(parts[2][at], start, 2 * head_size, main)
+                    tile = jnp.where(lane < head_size, low, jnp.where(lane < 2 * head_size, mid, high))
+                    mixed.append(tile)
+                at = starts[t]
+                items[h, 0, at : at + 2 * token_rows, :] = jnp.concatenate(mixed, axis=0).astype(BF16)
+                if t == 1:
+                    tails = [
+                        moved(values[at], start + main, rest * i, rest)
+                        for i, (values, at) in enumerate(
+                            ((held[...], one), (held[...], two), (parts[2], one), (parts[2], two))
+                        )
+                    ]
+                    tail = tails[3]
+                    for i in (2, 1, 0):
+                        tail = jnp.where(lane < rest * (i + 1), tails[i], tail)
+                    near, far = tail[: token_rows // 2], tail[token_rows // 2 :]
+                    tail = jnp.where(lane[: token_rows // 2] < half, near, pltpu.roll(far, half, 1))
+                    items[h, 0, at + 2 * token_rows :, :] = tail.astype(BF16)
         spread(item_copy(t))
-        got[t, me] = items[t, me]
+        span = pl.ds(starts[t], rows_of[t])
+        got[me, :, span] = items[me, :, span]
 
     token_scale = head_size ** (-0.5)
     tile = 16
@@ -537,7 +594,7 @@
     def token_attend(t):
         every_item(t).wait_recv()
         for unit in range(units):
-            packed = got[t, :, unit, pack * token_rows :, :].reshape(tokens, lanes)
+            packed = got[:, unit, pack * token_rows :, :].reshape(tokens, lanes)
 
             def one(block, c):
                 span = pl.ds(block * tile, tile)
@@ -548,8 +605,8 @@
                     if p == 0:
                         mine = (key_lane >= half) & (key_lane < half + head_size)
                     keys = jnp.where(mine, packed, jnp.zeros_like(packed))
-                    values = got[t, :, unit, at, :].reshape(tokens, lanes)
-                    q = got[t, span, unit, at, :].reshape(tile * token_rows, lanes)
+                    values = got[:, unit, at, :].reshape(tokens, lanes)
+                    q = got[span, unit, at, :].reshape(tile * token_rows, lanes)
                     scores = lax.dot_general(q, keys, LAST, preferred_element_type=F32)
                     scores = scores * token_scale + pair_buf[span].reshape(
                         tile * token_rows, tokens
@@ -568,6 +625,50 @@
         spread(out_copy(t))
         returned[t, me] = outs[t, me]
 
+    all_lane = lax.broadcasted_iota(jnp.int32, (tokens, lanes), 1)
+
+    def token_weights(t):
+        at = starts[t]
+        one = got[:, 0, at : at + token_rows, :].reshape(tokens, lanes)
+        two = got[:, 0, at + token_rows : at + 2 * token_rows, :].reshape(tokens, lanes)
+        bias = pair_buf[...].reshape(tokens, tokens)
+        for a, (q, k) in enumerate(((one, two), (two, one))):
+            mine = (all_lane >= a * head_size) & (all_lane < (a + 1) * head_size)
+            keys = jnp.where(mine, k, jnp.zeros_like(k))
+            scores = lax.dot_general(q, keys, LAST, preferred_element_type=F32)
+            scores = scores * token_scale + bias
+            expo = jnp.exp(scores - jnp.max(scores, -1, keepdims=True))
+            weights[t, a] = expo.astype(BF16)
+
+    def token_mix(t):
+        end = starts[1] + 2 * token_rows
+        tail = got[:, 0, end:, :].astype(F32)
+        flat = tail.reshape(n * token_rows // 2, lanes)
+        tail = jnp.concatenate(
+            [tail, pltpu.roll(flat, half, 1).reshape(tail.shape)], axis=1
+        ).reshape(tokens, lanes)
+        tail = jnp.where(all_lane < half, tail, 1.0).astype(BF16)
+        ratios = []
+        for a in range(2):
+            at = starts[t] + a * token_rows
+            values = got[:, 0, at : at + token_rows, :].reshape(tokens, lanes)
+            both = dot(weights[t, a], jnp.concatenate([values, tail], axis=1))
+            ratios.append(both / both[:, lanes + half : lanes + half + 1])
+        first, second = ratios
+        edge = rest * (2 * t + 1)
+        out = jnp.where(
+            all_lane >= 2 * head_size,
+            first[:, :lanes],
+            jnp.where(
+                all_lane >= half,
+                pltpu.roll(second[:, :lanes], lanes - main, 1),
+                jnp.where(all_lane < edge, first[:, lanes:], second[:, lanes:]),
+            ),
+        )
+        outs[t, :, 0, :, :] = out.astype(BF16).reshape(n, token_rows, lanes)
+        spread(out_copy(t))
+        returned[t, me] = outs[t, me]
+
     def token_finish(t):
         every_out(t).wait_recv()
         state = token_in[t * wave_rows : (t + 1) * wave_rows, :]
@@ -577,7 +678,13 @@
                 item = h * samples + t * wave_samples + a
                 owner, unit, p = item // per, item % per // pack - t * units, item % per % pack
                 block = returned[t, owner, unit]
-                if p == 1:
+                if waves == 2:
+                    block = block.astype(F32)
+                    to_main = pltpu.roll(block, (1 + a) * main, 1)
+                    shift = (main - rest * (2 * t + a)) % lanes
+                    to_rest = pltpu.roll(block, shift, 1) if shift else block
+                    block = jnp.where(lane < main, to_main, to_rest).astype(BF16)
+                elif p == 1:
                     block = pltpu.roll(block.astype(F32), half, 1).astype(BF16)
                 mix.append(block[:, :head_size])
             state = state + dot(
@@ -593,8 +700,16 @@
         token_project(t)
     loads["own_pair"].wait()
     every_pair().wait_recv()
-    for t in range(waves):
-        token_attend(t)
+    if waves == 1:
+        token_attend(0)
+    else:
+        for t in range(waves):
+            every_item(t).wait_recv()
+            token_weights(t)
+            if t == 0:
+                continue
+            for u in range(waves):
+                token_mix(u)
     loads["tout"].wait()
     for t in range(waves):
         token_finish(t)
@@ -734,8 +849,10 @@
             pltpu.VMEM((GROUPS, 2, gs, token_rows, channels), BF16),
             pltpu.VMEM((GROUPS, 2, gs, token_rows, channels), BF16),
             pltpu.VMEM((samples * token_rows, channels), F32),
-            pltpu.VMEM((waves, n, units, (pack + 1) * token_rows, 128), BF16),
-            pltpu.VMEM((waves, n, units, (pack + 1) * token_rows, 128), BF16),
+            pltpu.VMEM((n, units, sum(item_rows(token_rows, pack, waves)), 128), BF16),
+            pltpu.VMEM((n, units, sum(item_rows(token_rows, pack, waves)), 128), BF16),
+            pltpu.VMEM((2 * token_rows, channels), F32),
+            pltpu.VMEM((waves, 2, n * token_rows, n * token_rows), BF16),
             pltpu.VMEM((n, token_rows, n * token_rows), F32),
             pltpu.VMEM((waves, n, units, token_rows, 128), BF16),
             pltpu.VMEM((waves, n, units, token_rows, 128), BF16),

time: 49.5 us -> 50.5 us (1.020)
  Pallas kernels: 48.6 us -> 49.7 us
    pallas_call x1, Pallas kernels: 47.9 us -> 49 us  [shards(): pl.pallas_call(functools.partial(kernel, n), name='denoise', out_shape=(p...]
where the time goes in v3:
time: 50.5 us; the launch traced here: 50.3 us
  Pallas kernels  49.7 us (98%)
  between operations  0.65 us (1%)
    pallas_call x1, Pallas kernels, shards(): pl.pallas_call(functools.partial(kernel, n), name='denoise', out_shape=(p...  49 us

profile of v3, /device:TPU:1, one launch (start us, length us, event | category | flops | bytes accessed | tf_op | source)
XLA Modules:
  0.0 50.3 jit_solution(3105202627086531640)
XLA Ops:
  0.6 49.0 %denoise.1 = (f32[3,4,128]{2,1,0:T(4,128)S(1)}, f32[4,16,768]{2,1,0:T(8,128)S(1)}) custom-call(s32[4]{0:T(128)} %level_hbm.1, s32[2,4]{1,0:T(2,128)} %bitcast.5, f32[3,128]{1,0:T(4,128)} %x_true_hbm.1, f32[3,4,128]{2,1,0:T(4,128)} %bitcast.4, bf16[128,128]{1,0:T(8,128)(2,1)} %single_hbm.1, s32[1,128]{1,0:T(1,128)} %bitcast.6, f32[4,4,32,128]{3,2,1,0:T(8,128)} %bias_hbm.1, ...), custom_call_target="tpu_custom_call" | custom-call | tf_op jit(solution)/shard_map/denoise/pallas_call | solution.py:825
  49.6 0.7 %store.1 = (f32[3,4,128]{2,1,0:T(4,128)}, f32[4,16,768]{2,1,0:T(8,128)}) custom-call(f32[3,4,128]{2,1,0:T(4,128)S(1)} %get-tuple-element.6.denoised_ref, f32[4,16,768]{2,1,0:T(8,128)S(1)} %get-tuple-element.7.state_ref), custom_call_target="tpu_custom_call" | custom-call | tf_op jit(solution)/shard_map/store/pallas_call | solution.py:910

commit v4 on v3

--- a/solution.py
+++ b/solution.py
@@ -56,7 +56,7 @@
 def item_rows(token_rows, pack, waves):
     if waves == 1:
         return ((pack + 1) * token_rows,)
-    return 2 * token_rows, 2 * token_rows + token_rows // 2
+    return (2 * token_rows + token_rows // 2,) * 2
 
 
 def kernel(
@@ -101,8 +101,8 @@
     token_in,
     items,
     got,
-    held,
-    weights,
+    pair_own,
+    pair_out,
     pair_buf,
     outs,
     returned,
@@ -170,6 +170,7 @@
             ("atoms", single_hbm, single_ref),
             ("coord", w_coord_hbm, w_coord_ref),
             ("qkv", w_qkv_hbm, w_qkv_ref),
+            ("pair", pair_hbm, pair_own),
             ("atom_token", atom_token_hbm, atom_token_ref),
             ("edges", edges_hbm, edges_ref),
             ("bias", bias_hbm, bias_ref),
@@ -182,7 +183,6 @@
             ("back", w_back_hbm, w_back_ref),
             ("tout", w_tout_hbm, w_tout),
             ("final", w_final_hbm, w_final_ref),
-            ("own_pair", pair_hbm.at[own_head], pair_buf.at[me]),
         )
     ):
         loads[name] = pltpu.make_async_copy(src, dst, load_sem.at[slot])
@@ -355,20 +355,14 @@
             attend(first, g)
             project(first + 1, g)
             send_halo(first + 1, g)
-            if first == 0:
-                pair_batch(g)
             return c
 
         lax.fori_loop(0, GROUPS, step, 0)
+        if first == 0:
+            lax.fori_loop(1, n, pair_start, 0)
 
         def last(g, c):
             finish(g, attend(first + 1, g))
-            if first == 0:
-
-                @pl.when(g == 0)
-                def _():
-                    pair_batch(2)
-
             return c
 
         lax.fori_loop(0, GROUPS, last, 0)
@@ -393,7 +387,7 @@
 
     def pair_copy(target, slot):
         return remote(
-            pair_hbm.at[(target * per) // samples],
+            pair_out.at[(target * per) // samples],
             pair_buf.at[slot],
             pair_send,
             pair_recv,
@@ -404,12 +398,10 @@
         pair_copy(lax.rem(me + k, n), me).start()
         return c
 
-    third = (n - 1) // 3
-
-    def pair_batch(number):
-        low = 1 + number * third
-        high = jnp.where(number == 2, n, low + third)
-        lax.fori_loop(low, high, pair_start, 0)
+    loads["pair"].wait()
+    rows = pair_own[...]
+    pair_out[...] = (rows - jnp.max(rows, -1, keepdims=True)).astype(BF16)
+    pair_buf[me] = pair_out[own_head]
 
     def pool(g, value):
         pooled = jnp.maximum(dot(normed(value).astype(BF16), w_pool_ref[...]), 0.0)
@@ -555,8 +547,6 @@
                 key = keys[0] if pack == 1 else jnp.where(lane < half, keys[1], keys[0])
                 items[owner, unit, pack * token_rows :, :] = key.astype(BF16)
         if waves == 2:
-            if t == 0:
-                held[...] = parts[2]
             one, two = slice(0, token_rows), slice(token_rows, 2 * token_rows)
             for h in range(heads):
                 start = h * head_size
@@ -569,19 +559,14 @@
                     mixed.append(tile)
                 at = starts[t]
                 items[h, 0, at : at + 2 * token_rows, :] = jnp.concatenate(mixed, axis=0).astype(BF16)
-                if t == 1:
-                    tails = [
-                        moved(values[at], start + main, rest * i, rest)
-                        for i, (values, at) in enumerate(
-                            ((held[...], one), (held[...], two), (parts[2], one), (parts[2], two))
-                        )
-                    ]
-                    tail = tails[3]
-                    for i in (2, 1, 0):
-                        tail = jnp.where(lane < rest * (i + 1), tails[i], tail)
-                    near, far = tail[: token_rows // 2], tail[token_rows // 2 :]
-                    tail = jnp.where(lane[: token_rows // 2] < half, near, pltpu.roll(far, half, 1))
-                    items[h, 0, at + 2 * token_rows :, :] = tail.astype(BF16)
+                tail = jnp.where(
+                    lane < rest,
+                    moved(parts[2][one], start + main, 0, rest),
+                    moved(parts[2][two], start + main, half - rest, rest),
+                )
+                near, far = tail[: token_rows // 2], tail[token_rows // 2 :]
+                tail = jnp.where(lane[: token_rows // 2] < half, near, pltpu.roll(far, half, 1))
+                items[h, 0, at + 2 * token_rows : at + rows_of[t], :] = tail.astype(BF16)
         spread(item_copy(t))
         span = pl.ds(starts[t], rows_of[t])
         got[me, :, span] = items[me, :, span]
@@ -608,7 +593,7 @@
                     values = got[:, unit, at, :].reshape(tokens, lanes)
                     q = got[span, unit, at, :].reshape(tile * token_rows, lanes)
                     scores = lax.dot_general(q, keys, LAST, preferred_element_type=F32)
-                    scores = scores * token_scale + pair_buf[span].reshape(
+                    scores = scores * token_scale + pair_buf[span].astype(F32).reshape(
                         tile * token_rows, tokens
                     )
                     expo = jnp.exp(scores - jnp.max(scores, -1, keepdims=True)).astype(BF16)
@@ -627,42 +612,39 @@
 
     all_lane = lax.broadcasted_iota(jnp.int32, (tokens, lanes), 1)
 
-    def token_weights(t):
+    def token_pair(t):
+        every_item(t).wait_recv()
         at = starts[t]
         one = got[:, 0, at : at + token_rows, :].reshape(tokens, lanes)
         two = got[:, 0, at + token_rows : at + 2 * token_rows, :].reshape(tokens, lanes)
-        bias = pair_buf[...].reshape(tokens, tokens)
+        tail = got[:, 0, at + 2 * token_rows : at + rows_of[t], :].astype(F32)
+        flat = tail.reshape(n * token_rows // 2, lanes)
+        tail = jnp.concatenate(
+            [tail, pltpu.roll(flat, half, 1).reshape(tail.shape)], axis=1
+        ).reshape(tokens, lanes)
+        tail = jnp.where(all_lane < half, tail, 1.0).astype(BF16)
+        bias = pair_buf[...].astype(F32).reshape(tokens, tokens)
+        ratios = []
         for a, (q, k) in enumerate(((one, two), (two, one))):
             mine = (all_lane >= a * head_size) & (all_lane < (a + 1) * head_size)
             keys = jnp.where(mine, k, jnp.zeros_like(k))
             scores = lax.dot_general(q, keys, LAST, preferred_element_type=F32)
             scores = scores * token_scale + bias
-            expo = jnp.exp(scores - jnp.max(scores, -1, keepdims=True))
-            weights[t, a] = expo.astype(BF16)
-
-    def token_mix(t):
-        end = starts[1] + 2 * token_rows
-        tail = got[:, 0, end:, :].astype(F32)
-        flat = tail.reshape(n * token_rows // 2, lanes)
-        tail = jnp.concatenate(
-            [tail, pltpu.roll(flat, half, 1).reshape(tail.shape)], axis=1
-        ).reshape(tokens, lanes)
-        tail = jnp.where(all_lane < half, tail, 1.0).astype(BF16)
-        ratios = []
-        for a in range(2):
-            at = starts[t] + a * token_rows
-            values = got[:, 0, at : at + token_rows, :].reshape(tokens, lanes)
-            both = dot(weights[t, a], jnp.concatenate([values, tail], axis=1))
+            expo = jnp.exp(scores - jnp.max(scores, -1, keepdims=True)).astype(BF16)
+            both = dot(expo, jnp.concatenate([q, tail], axis=1))
             ratios.append(both / both[:, lanes + half : lanes + half + 1])
         first, second = ratios
-        edge = rest * (2 * t + 1)
         out = jnp.where(
-            all_lane >= 2 * head_size,
+            all_lane >= lanes - main,
             first[:, :lanes],
             jnp.where(
-                all_lane >= half,
-                pltpu.roll(second[:, :lanes], lanes - main, 1),
-                jnp.where(all_lane < edge, first[:, lanes:], second[:, lanes:]),
+                all_lane < rest,
+                first[:, lanes:],
+                jnp.where(
+                    all_lane < half - rest,
+                    pltpu.roll(second[:, :lanes], half - rest, 1),
+                    second[:, lanes:],
+                ),
             ),
         )
         outs[t, :, 0, :, :] = out.astype(BF16).reshape(n, token_rows, lanes)
@@ -679,11 +661,8 @@
                 owner, unit, p = item // per, item % per // pack - t * units, item % per % pack
                 block = returned[t, owner, unit]
                 if waves == 2:
-                    block = block.astype(F32)
-                    to_main = pltpu.roll(block, (1 + a) * main, 1)
-                    shift = (main - rest * (2 * t + a)) % lanes
-                    to_rest = pltpu.roll(block, shift, 1) if shift else block
-                    block = jnp.where(lane < main, to_main, to_rest).astype(BF16)
+                    shift = lanes - rest if a else main
+                    block = pltpu.roll(block.astype(F32), shift, 1).astype(BF16)
                 elif p == 1:
                     block = pltpu.roll(block.astype(F32), half, 1).astype(BF16)
                 mix.append(block[:, :head_size])
@@ -698,18 +677,12 @@
     loads["tqkv"].wait()
     for t in range(waves):
         token_project(t)
-    loads["own_pair"].wait()
     every_pair().wait_recv()
     if waves == 1:
         token_attend(0)
     else:
         for t in range(waves):
-            every_item(t).wait_recv()
-            token_weights(t)
-            if t == 0:
-                continue
-            for u in range(waves):
-                token_mix(u)
+            token_pair(t)
     loads["tout"].wait()
     for t in range(waves):
         token_finish(t)
@@ -851,9 +824,9 @@
             pltpu.VMEM((samples * token_rows, channels), F32),
             pltpu.VMEM((n, units, sum(item_rows(token_rows, pack, waves)), 128), BF16),
             pltpu.VMEM((n, units, sum(item_rows(token_rows, pack, waves)), 128), BF16),
-            pltpu.VMEM((2 * token_rows, channels), F32),
-            pltpu.VMEM((waves, 2, n * token_rows, n * token_rows), BF16),
-            pltpu.VMEM((n, token_rows, n * token_rows), F32),
+            pltpu.VMEM(pair_bias.shape, F32),
+            pltpu.VMEM(pair_bias.shape, BF16),
+            pltpu.VMEM((n, token_rows, n * token_rows), BF16),
             pltpu.VMEM((waves, n, units, token_rows, 128), BF16),
             pltpu.VMEM((waves, n, units, token_rows, 128), BF16),
             pltpu.VMEM((waves, 3, samples // waves * token_rows, width), BF16),

time: 50.5 us -> 47.2 us (0.935)
  Pallas kernels: 49.7 us -> 46.4 us
    pallas_call x1, Pallas kernels: 49 us -> 45.7 us  [shards(): pl.pallas_call(functools.partial(kernel, n), name='denoise', out_shape=(p...]
where the time goes in v4:
time: 47.2 us; the launch traced here: 47 us
  Pallas kernels  46.4 us (98%)
  between operations  0.65 us (1%)
    pallas_call x1, Pallas kernels, shards(): pl.pallas_call(functools.partial(kernel, n), name='denoise', out_shape=(p...  45.7 us

profile of v4, /device:TPU:1, one launch (start us, length us, event | category | flops | bytes accessed | tf_op | source)
XLA Modules:
  0.0 47.0 jit_solution(15492847411633834602)
XLA Ops:
  0.6 45.7 %denoise.1 = (f32[3,4,128]{2,1,0:T(4,128)S(1)}, f32[4,16,768]{2,1,0:T(8,128)S(1)}) custom-call(s32[4]{0:T(128)} %level_hbm.1, s32[2,4]{1,0:T(2,128)} %bitcast.5, f32[3,128]{1,0:T(4,128)} %x_true_hbm.1, f32[3,4,128]{2,1,0:T(4,128)} %bitcast.4, bf16[128,128]{1,0:T(8,128)(2,1)} %single_hbm.1, s32[1,128]{1,0:T(1,128)} %bitcast.6, f32[4,4,32,128]{3,2,1,0:T(8,128)} %bias_hbm.1, ...), custom_call_target="tpu_custom_call" | custom-call | tf_op jit(solution)/shard_map/denoise/pallas_call | solution.py:798
  46.3 0.7 %store.1 = (f32[3,4,128]{2,1,0:T(4,128)}, f32[4,16,768]{2,1,0:T(8,128)}) custom-call(f32[3,4,128]{2,1,0:T(4,128)S(1)} %get-tuple-element.6.denoised_ref, f32[4,16,768]{2,1,0:T(8,128)S(1)} %get-tuple-element.7.state_ref), custom_call_target="tpu_custom_call" | custom-call | tf_op jit(solution)/shard_map/store/pallas_call | solution.py:883

commit v5 on v4

--- a/solution.py
+++ b/solution.py
@@ -51,6 +51,13 @@
     pack = 2 if per % 2 == 0 else 1
     waves = GROUPS if per == samples and gs == pack else 1
     return per, pack, waves, per // pack // waves
+
+
+def reach_rounds(n):
+    rounds, known = 0, 1
+    while known < n - 1:
+        rounds, known = rounds + 1, 2 * known
+    return rounds
 
 
 def item_rows(token_rows, pack, waves):
@@ -91,6 +98,8 @@
     w_coord_ref,
     w_final_ref,
     stream,
+    edge,
+    near_token,
     kv,
     queries,
     masked_bias,
@@ -118,6 +127,7 @@
     w_pool_ref,
     w_back_ref,
     load_sem,
+    ready,
     halo_send,
     halo_recv,
     count_send,
@@ -132,6 +142,10 @@
     out_recv,
     back_send,
     back_recv,
+    edge_send,
+    edge_recv,
+    token_send,
+    token_recv,
 ):
     samples = noise_ref.shape[1]
     atom_rows, width = single_ref.shape
@@ -154,11 +168,26 @@
 
     barrier = pltpu.get_barrier_semaphore()
 
-    def greet(k, c):
-        pl.semaphore_signal(
-            barrier, inc=1, device_id={"seq": lax.rem(me + k, n)}, device_id_type=MESH
-        )
-        return c
+    def signal(semaphore, reach):
+        for there, target in ((me >= reach, me - reach), (me + reach < n, me + reach)):
+
+            @pl.when(there)
+            def _():
+                pl.semaphore_signal(
+                    semaphore, inc=1, device_id={"seq": target}, device_id_type=MESH
+                )
+
+    def await_signals(semaphore, reach):
+        count = (me >= reach).astype(jnp.int32) + (me + reach < n).astype(jnp.int32)
+        pl.semaphore_wait(semaphore, count)
+
+    rounds = reach_rounds(n)
+
+    def met(number):
+        if number < rounds:
+            await_signals(ready.at[number], 2**number)
+        if number + 1 < rounds:
+            signal(ready.at[number + 1], 2 ** (number + 1))
 
     own_head = (me * per) // samples
     loads = {}
@@ -188,7 +217,7 @@
         loads[name] = pltpu.make_async_copy(src, dst, load_sem.at[slot])
         loads[name].start()
         if name == "qkv":
-            lax.fori_loop(1, n, greet, 0)
+            signal(barrier, 1)
 
     upper_root = 160.0 ** (1.0 / 7.0)
     lower_root = 0.0004 ** (1.0 / 7.0)
@@ -222,7 +251,7 @@
         for c in range(3):
             at = 3 * s + c
             value = value + columns[:, at : at + 1] * w_coord_ref[c : c + 1, :]
-        stream[s // gs, pl.ds((s % gs) * atom_rows, atom_rows), :] = value
+        stream[s // gs, s % gs] = value
 
     def exchange(to_right, to_left, begin):
         if begin:
@@ -273,7 +302,7 @@
         )
 
     def project(layer, g):
-        normal_in = normed(stream[g]).astype(BF16)
+        normal_in = normed(stream[g].reshape(gs * atom_rows, width)).astype(BF16)
         key_value = dot(normal_in, w_qkv_ref[layer, :, width:]).astype(BF16)
         for i in range(gs):
             kv[layer, g, i, RIM : RIM + atom_rows, :] = key_value[
@@ -293,7 +322,8 @@
     ones = jnp.ones((KEY_WINDOW, width), BF16)
 
     def attend(layer, g):
-        exchange(*halo(layer, g), False)
+        if layer != ENC_LAYERS:
+            exchange(*halo(layer, g), False)
         mixed = []
         pairs = [(i, b) for i in range(gs) for b in range(blocks)]
         for start in range(0, len(pairs), 8):
@@ -321,13 +351,13 @@
                     below = jnp.where(few_lanes == h, rows[:, width:], below)
                 mixed.append((number / below).astype(BF16))
         mixed = jnp.concatenate(mixed, axis=0)
-        value = stream[g] + dot(mixed, w_out_ref[layer])
+        value = stream[g].reshape(gs * atom_rows, width) + dot(mixed, w_out_ref[layer])
         normal_mid = normed(value).astype(BF16)
         gated = dot(normal_mid, w_up_ref[layer])
         gate = gated[:, : 2 * width]
         hidden = (gate / (1.0 + jnp.exp(-gate)) * gated[:, 2 * width :]).astype(BF16)
         value = value + dot(hidden, w_down_ref[layer])
-        stream[g] = value
+        stream[g] = value.reshape(gs, atom_rows, width)
         return value
 
     def pool_copy(g):
@@ -344,21 +374,91 @@
             remote(counts.at[0], counts.at[4], count_send.at[1], count_recv.at[1], left),
         )
 
+    def edge_copy(g):
+        return (
+            remote(
+                stream.at[g, :, pl.ds(atom_rows - RIM, RIM), :],
+                edge.at[0, g],
+                edge_send.at[0],
+                edge_recv.at[g, 0],
+                right,
+            ),
+            remote(
+                stream.at[g, :, pl.ds(0, RIM), :],
+                edge.at[1, g],
+                edge_send.at[1],
+                edge_recv.at[g, 1],
+                left,
+            ),
+        )
+
+    def token_copy():
+        return (
+            remote(atom_token_ref, near_token.at[0], token_send.at[0], token_recv.at[0], right),
+            remote(atom_token_ref, near_token.at[1], token_send.at[1], token_recv.at[1], left),
+        )
+
+    def selects(row):
+        spot = row - (me - 1) * token_rows
+        return (
+            lax.broadcasted_iota(jnp.int32, (3 * token_rows, atom_rows), 0) == spot
+        ).astype(F32)
+
     def back_copy(t):
         return (
             remote(back.at[t, 1], back.at[t, 0], back_send.at[0], back_recv.at[t, 0], right),
             remote(back.at[t, 1], back.at[t, 2], back_send.at[1], back_recv.at[t, 1], left),
         )
 
+    def take_back(g):
+        t, base = (g, 0) if waves == GROUPS else (0, g * gs * token_rows)
+        if waves == GROUPS:
+            exchange(*back_copy(t), False)
+        else:
+
+            @pl.when(g == 0)
+            def _():
+                exchange(*back_copy(0), False)
+
+        exchange(*edge_copy(g), False)
+        beyond = []
+        for i in range(gs):
+            span = pl.ds(pl.multiple_of(base + i * token_rows, token_rows), token_rows)
+            near = jnp.concatenate([back[t, j, span, :] for j in range(3)], axis=0)
+            stream[g, i] += lax.dot_general(sel, near, FIRST, preferred_element_type=F32)
+            for side, rows in ((0, slice(atom_rows - RIM, atom_rows)), (1, slice(0, RIM))):
+                picked = lax.dot_general(
+                    near_sel[side], near, FIRST, preferred_element_type=F32
+                )
+                beyond.append(edge[side, g, i] + picked[rows])
+        project(ENC_LAYERS, g)
+        normal = normed(jnp.concatenate(beyond, axis=0)).astype(BF16)
+        key_value = dot(normal, w_qkv_ref[ENC_LAYERS, :, width:]).astype(BF16)
+        for i in range(gs):
+            at = 2 * i * RIM
+            kv[ENC_LAYERS, g, i, 0:RIM, :] = key_value[at : at + RIM]
+            kv[ENC_LAYERS, g, i, RIM + atom_rows :, :] = key_value[at + RIM : at + 2 * RIM]
+
     def run_pair(first, finish):
         def step(g, c):
+            if first == ENC_LAYERS:
+                take_back(g)
             attend(first, g)
             project(first + 1, g)
             send_halo(first + 1, g)
+            if first == 0:
+                for group in range(GROUPS):
+
+                    @pl.when(g == group)
+                    def _():
+                        met(2 + group)
+
             return c
 
         lax.fori_loop(0, GROUPS, step, 0)
         if first == 0:
+            for number in range(2 + GROUPS, rounds):
+                met(number)
             lax.fori_loop(1, n, pair_start, 0)
 
         def last(g, c):
@@ -369,21 +469,21 @@
 
     loads["qkv"].wait()
     project(0, 0)
-    pl.semaphore_wait(barrier, n - 1)
+    await_signals(barrier, 1)
+    signal(ready.at[0], 1)
     send_halo(0, 0)
     project(0, 1)
     send_halo(0, 1)
+    met(0)
     loads["atom_token"].wait()
-    relative = atom_token_ref[...] - (me - 1) * token_rows
-    selector = (
-        lax.broadcasted_iota(jnp.int32, (3 * token_rows, atom_rows), 0) == relative
-    ).astype(F32)
+    selector = selects(atom_token_ref[...])
     sel = selector.astype(BF16)
     counted = jnp.broadcast_to(jnp.sum(selector, 1, keepdims=True), (3 * token_rows, 128))
     for j in range(3):
         counts[j] = counted[j * token_rows : (j + 1) * token_rows].astype(BF16)
 
     exchange(*count_copy(), True)
+    exchange(*token_copy(), True)
 
     def pair_copy(target, slot):
         return remote(
@@ -414,6 +514,7 @@
             own_sum[g, i] = part[token_rows : 2 * token_rows]
             psend[g, 1, i] = part[2 * token_rows :].astype(BF16)
         exchange(*pool_copy(g), True)
+        exchange(*edge_copy(g), True)
 
     loads["bias"].wait()
     loads["edges"].wait()
@@ -435,6 +536,8 @@
         for t in range(waves):
             back[t, 0] = jnp.zeros(back.shape[2:], BF16)
         counts[3] = jnp.zeros(counts.shape[1:], BF16)
+        edge[0] = jnp.zeros(edge.shape[1:], F32)
+        near_token[0] = jnp.full((1, atom_rows), -tokens, jnp.int32)
 
     @pl.when(jnp.logical_not(has_right))
     def _():
@@ -446,9 +549,12 @@
         for t in range(waves):
             back[t, 2] = jnp.zeros(back.shape[2:], BF16)
         counts[4] = jnp.zeros(counts.shape[1:], BF16)
+        edge[1] = jnp.zeros(edge.shape[1:], F32)
+        near_token[1] = jnp.full((1, atom_rows), -tokens, jnp.int32)
 
     for name in ("out", "up", "down", "pool"):
         loads[name].wait()
+    met(1)
     run_pair(0, pool)
     loads["single"].wait()
     loads["back"].wait()
@@ -477,7 +583,8 @@
 
     def spread(copy_of):
         def step(k, c):
-            copy_of(lax.rem(me + k, n), me).start()
+            turn = lax.rem(k + n // 2 - 1, n - 1) + 1
+            copy_of(lax.rem(me + turn, n), me).start()
             return c
 
         lax.fori_loop(1, n, step, 0)
@@ -687,18 +794,6 @@
     for t in range(waves):
         token_finish(t)
     first = ENC_LAYERS
-    for g in range(GROUPS):
-        for t in range(waves):
-            if g * waves // GROUPS == t and (waves == GROUPS or g == 0):
-                exchange(*back_copy(t), False)
-        for i in range(gs):
-            s = g * gs + i
-            t, at = s // wave_samples, s % wave_samples * token_rows
-            near = jnp.concatenate([back[t, j, at : at + token_rows, :] for j in range(3)], axis=0)
-            picked = lax.dot_general(sel, near, FIRST, preferred_element_type=F32)
-            stream[g, i * atom_rows : (i + 1) * atom_rows, :] += picked
-        project(first, g)
-        send_halo(first, g)
 
     def finish(g, value):
         normal = normed(value).astype(BF16)
@@ -719,25 +814,36 @@
                 denoised_ref[c, pl.ds(s, 1), :] = result[c : c + 1]
 
     loads["final"].wait()
-    run_pair(first, finish)
-
+    exchange(*token_copy(), False)
     sent(
         remote(
-            kv.at[:, :, :, pl.ds(0, RIM), :],
-            kv.at[:, :, :, pl.ds(0, RIM), :],
+            stream.at[:, :, pl.ds(0, RIM), :], edge.at[0], edge_send.at[0], edge_recv.at[0, 0], right
+        ),
+        remote(
+            stream.at[:, :, pl.ds(0, RIM), :], edge.at[1], edge_send.at[1], edge_recv.at[0, 1], left
+        ),
+    )
+    near_sel = [selects(near_token[side]).astype(BF16) for side in range(2)]
+    run_pair(first, finish)
+
+    sent(
+        remote(
+            kv.at[pl.ds(0, LAYERS - 1), :, :, pl.ds(0, RIM), :],
+            kv.at[pl.ds(0, LAYERS - 1), :, :, pl.ds(0, RIM), :],
             halo_send.at[0],
             halo_recv.at[0, 0, 0],
             right,
         ),
         remote(
-            kv.at[:, :, :, pl.ds(0, RIM), :],
-            kv.at[:, :, :, pl.ds(0, RIM), :],
+            kv.at[pl.ds(0, LAYERS - 1), :, :, pl.ds(0, RIM), :],
+            kv.at[pl.ds(0, LAYERS - 1), :, :, pl.ds(0, RIM), :],
             halo_send.at[1],
             halo_recv.at[0, 0, 1],
             left,
         ),
     )
     sent(*count_copy())
+    sent(*token_copy())
     sent(
         remote(psend.at[:, 1], precv.at[:, 0], pool_send.at[0], pool_recv.at[0, 0], right),
         remote(psend.at[:, 0], precv.at[:, 1], pool_send.at[1], pool_recv.at[0, 1], left),
@@ -813,7 +919,9 @@
             pltpu.VMEM((1, atom_rows), jnp.int32),
             pltpu.VMEM(w_coord.shape, F32),
             pltpu.VMEM(w_final.shape, BF16),
-            pltpu.VMEM((GROUPS, gs * atom_rows, width), F32),
+            pltpu.VMEM((GROUPS, gs, atom_rows, width), F32),
+            pltpu.VMEM((2, GROUPS, gs, RIM, width), F32),
+            pltpu.VMEM((2, 1, atom_rows), jnp.int32),
             pltpu.VMEM((LAYERS, GROUPS, gs, atom_rows + 2 * RIM, 2 * width), BF16),
             pltpu.VMEM((GROUPS, gs * atom_rows, width), BF16),
             pltpu.VMEM((blocks, atom_heads * QUERY_BLOCK, KEY_WINDOW), F32),
@@ -841,6 +949,7 @@
             pltpu.VMEM(w_pool.shape, BF16),
             pltpu.VMEM(w_back.shape, BF16),
             dma((19,)),
+            pltpu.SemaphoreType.REGULAR((reach_rounds(n),)),
             dma((2,)),
             dma((LAYERS, GROUPS, 2)),
             dma((2,)),
@@ -855,6 +964,10 @@
             dma((waves,)),
             dma((2,)),
             dma((waves, 2)),
+            dma((2,)),
+            dma((GROUPS, 2)),
+            dma((2,)),
+            dma((2,)),
         ],
         compiler_params=pltpu.CompilerParams(
             collective_id=0, has_side_effects=True, vmem_limit_bytes=56 * 1024 * 1024

time: 47.2 us -> 43.4 us (0.919)
  Pallas kernels: 46.4 us -> 42.6 us
    pallas_call x1, Pallas kernels: 45.7 us -> 41.9 us  [shards(): pl.pallas_call(functools.partial(kernel, n), name='denoise', out_shape=(p...]
where the time goes in v5:
time: 43.4 us; the launch traced here: 43.2 us
  Pallas kernels  42.6 us (98%)
  between operations  0.65 us (1%)
    pallas_call x1, Pallas kernels, shards(): pl.pallas_call(functools.partial(kernel, n), name='denoise', out_shape=(p...  41.9 us

profile of v5, /device:TPU:1, one launch (start us, length us, event | category | flops | bytes accessed | tf_op | source)
XLA Modules:
  0.0 43.2 jit_solution(6600881532216352745)
XLA Ops:
  0.6 41.9 %denoise.1 = (f32[3,4,128]{2,1,0:T(4,128)S(1)}, f32[4,16,768]{2,1,0:T(8,128)S(1)}) custom-call(s32[4]{0:T(128)} %level_hbm.1, s32[2,4]{1,0:T(2,128)} %bitcast.5, f32[3,128]{1,0:T(4,128)} %x_true_hbm.1, f32[3,4,128]{2,1,0:T(4,128)} %bitcast.4, bf16[128,128]{1,0:T(8,128)(2,1)} %single_hbm.1, s32[1,128]{1,0:T(1,128)} %bitcast.6, f32[4,4,32,128]{3,2,1,0:T(8,128)} %bias_hbm.1, ...), custom_call_target="tpu_custom_call" | custom-call | tf_op jit(solution)/shard_map/denoise/pallas_call | solution.py:904
  42.5 0.7 %store.1 = (f32[3,4,128]{2,1,0:T(4,128)}, f32[4,16,768]{2,1,0:T(8,128)}) custom-call(f32[3,4,128]{2,1,0:T(4,128)S(1)} %get-tuple-element.6.denoised_ref, f32[4,16,768]{2,1,0:T(8,128)S(1)} %get-tuple-element.7.state_ref), custom_call_target="tpu_custom_call" | custom-call | tf_op jit(solution)/shard_map/store/pallas_call | solution.py:996

commit v6 on v5

--- a/solution.py
+++ b/solution.py
@@ -182,6 +182,12 @@
         pl.semaphore_wait(semaphore, count)
 
     rounds = reach_rounds(n)
+    side = 4 if n % 4 == 0 else 1
+
+    def far_first(k):
+        plane = k // side
+        plane = lax.rem(me // side + (n // side) // 2 + plane, n // side)
+        return plane * side + lax.rem(me + k, side)
 
     def met(number):
         if number < rounds:
@@ -583,11 +589,15 @@
 
     def spread(copy_of):
         def step(k, c):
-            turn = lax.rem(k + n // 2 - 1, n - 1) + 1
-            copy_of(lax.rem(me + turn, n), me).start()
+            target = far_first(k)
+
+            @pl.when(target != me)
+            def _():
+                copy_of(target, me).start()
+
             return c
 
-        lax.fori_loop(1, n, step, 0)
+        lax.fori_loop(0, n, step, 0)
 
     others = pl.ds(0, n - 1)
 
@@ -761,16 +771,28 @@
     def token_finish(t):
         every_out(t).wait_recv()
         state = token_in[t * wave_rows : (t + 1) * wave_rows, :]
-        for h in range(heads):
+        if waves == 2:
+            samples_mixed = []
+            for a in range(wave_samples):
+                begin = half - main - rest if a else lanes - main
+                tiles = [None] * (channels // lanes)
+                for h in range(heads):
+                    low = h * head_size
+                    block = returned[t, h, 0].astype(F32)
+                    turned = pltpu.roll(block, (low - begin) % lanes, 1)
+                    for j in range(low // lanes, (low + head_size - 1) // lanes + 1):
+                        above = lane + j * lanes >= low
+                        tiles[j] = turned if tiles[j] is None else jnp.where(above, turned, tiles[j])
+                samples_mixed.append(jnp.concatenate(tiles, axis=1))
+            mixed = jnp.concatenate(samples_mixed, axis=0).astype(BF16)
+            state = state + dot(mixed, w_tout[...])
+        for h in range(heads) if waves == 1 else ():
             mix = []
             for a in range(wave_samples):
                 item = h * samples + t * wave_samples + a
                 owner, unit, p = item // per, item % per // pack - t * units, item % per % pack
                 block = returned[t, owner, unit]
-                if waves == 2:
-                    shift = lanes - rest if a else main
-                    block = pltpu.roll(block.astype(F32), shift, 1).astype(BF16)
-                elif p == 1:
+                if p == 1:
                     block = pltpu.roll(block.astype(F32), half, 1).astype(BF16)
                 mix.append(block[:, :head_size])
             state = state + dot(

time: 43.4 us -> 43.3 us (level)
  no operation moved by 1% of the time
where the time goes in v6:
time: 43.3 us; the launch traced here: 43.1 us
  Pallas kernels  42.5 us (98%)
  between operations  0.65 us (2%)
    pallas_call x1, Pallas kernels, shards(): pl.pallas_call(functools.partial(kernel, n), name='denoise', out_shape=(p...  41.8 us

profile of v6, /device:TPU:1, one launch (start us, length us, event | category | flops | bytes accessed | tf_op | source)
XLA Modules:
  0.0 43.1 jit_solution(10016957289104264485)
XLA Ops:
  0.6 41.8 %denoise.1 = (f32[3,4,128]{2,1,0:T(4,128)S(1)}, f32[4,16,768]{2,1,0:T(8,128)S(1)}) custom-call(s32[4]{0:T(128)} %level_hbm.1, s32[2,4]{1,0:T(2,128)} %bitcast.5, f32[3,128]{1,0:T(4,128)} %x_true_hbm.1, f32[3,4,128]{2,1,0:T(4,128)} %bitcast.4, bf16[128,128]{1,0:T(8,128)(2,1)} %single_hbm.1, s32[1,128]{1,0:T(1,128)} %bitcast.6, f32[4,4,32,128]{3,2,1,0:T(8,128)} %bias_hbm.1, ...), custom_call_target="tpu_custom_call" | custom-call | tf_op jit(solution)/shard_map/denoise/pallas_call | solution.py:926
  42.4 0.7 %store.1 = (f32[3,4,128]{2,1,0:T(4,128)}, f32[4,16,768]{2,1,0:T(8,128)}) custom-call(f32[3,4,128]{2,1,0:T(4,128)S(1)} %get-tuple-element.6.denoised_ref, f32[4,16,768]{2,1,0:T(8,128)S(1)} %get-tuple-element.7.state_ref), custom_call_target="tpu_custom_call" | custom-call | tf_op jit(solution)/shard_map/store/pallas_call | solution.py:1018

commit v7 on v6

--- a/solution.py
+++ b/solution.py
@@ -99,6 +99,7 @@
     w_final_ref,
     stream,
     edge,
+    rim,
     near_token,
     kv,
     queries,
@@ -184,10 +185,14 @@
     rounds = reach_rounds(n)
     side = 4 if n % 4 == 0 else 1
 
-    def far_first(k):
-        plane = k // side
-        plane = lax.rem(me // side + (n // side) // 2 + plane, n // side)
-        return plane * side + lax.rem(me + k, side)
+    planes = n // side
+
+    def far_first():
+        for k in range(n):
+            offset = (planes // 2 + k // side) % planes
+            if offset or k % side:
+                plane = lax.rem(me // side + offset, planes)
+                yield plane * side + lax.rem(me + k, side)
 
     def met(number):
         if number < rounds:
@@ -252,7 +257,7 @@
     loads["atoms"].wait()
     loads["coord"].wait()
     single = single_ref[...].astype(F32)
-    for s in range(samples):
+    def embed(s):
         value = single
         for c in range(3):
             at = 3 * s + c
@@ -383,14 +388,14 @@
     def edge_copy(g):
         return (
             remote(
-                stream.at[g, :, pl.ds(atom_rows - RIM, RIM), :],
+                rim.at[0, g],
                 edge.at[0, g],
                 edge_send.at[0],
                 edge_recv.at[g, 0],
                 right,
             ),
             remote(
-                stream.at[g, :, pl.ds(0, RIM), :],
+                rim.at[1, g],
                 edge.at[1, g],
                 edge_send.at[1],
                 edge_recv.at[g, 1],
@@ -436,7 +441,7 @@
                 picked = lax.dot_general(
                     near_sel[side], near, FIRST, preferred_element_type=F32
                 )
-                beyond.append(edge[side, g, i] + picked[rows])
+                beyond.append(edge[side, g, i].astype(F32) + picked[rows])
         project(ENC_LAYERS, g)
         normal = normed(jnp.concatenate(beyond, axis=0)).astype(BF16)
         key_value = dot(normal, w_qkv_ref[ENC_LAYERS, :, width:]).astype(BF16)
@@ -473,11 +478,15 @@
 
         lax.fori_loop(0, GROUPS, last, 0)
 
+    for s in range(gs):
+        embed(s)
     loads["qkv"].wait()
     project(0, 0)
     await_signals(barrier, 1)
     signal(ready.at[0], 1)
     send_halo(0, 0)
+    for s in range(gs, samples):
+        embed(s)
     project(0, 1)
     send_halo(0, 1)
     met(0)
@@ -520,6 +529,9 @@
             own_sum[g, i] = part[token_rows : 2 * token_rows]
             psend[g, 1, i] = part[2 * token_rows :].astype(BF16)
         exchange(*pool_copy(g), True)
+        for i in range(gs):
+            rim[0, g, i] = stream[g, i, atom_rows - RIM :, :].astype(BF16)
+            rim[1, g, i] = stream[g, i, :RIM, :].astype(BF16)
         exchange(*edge_copy(g), True)
 
     loads["bias"].wait()
@@ -542,7 +554,7 @@
         for t in range(waves):
             back[t, 0] = jnp.zeros(back.shape[2:], BF16)
         counts[3] = jnp.zeros(counts.shape[1:], BF16)
-        edge[0] = jnp.zeros(edge.shape[1:], F32)
+        edge[0] = jnp.zeros(edge.shape[1:], BF16)
         near_token[0] = jnp.full((1, atom_rows), -tokens, jnp.int32)
 
     @pl.when(jnp.logical_not(has_right))
@@ -555,7 +567,7 @@
         for t in range(waves):
             back[t, 2] = jnp.zeros(back.shape[2:], BF16)
         counts[4] = jnp.zeros(counts.shape[1:], BF16)
-        edge[1] = jnp.zeros(edge.shape[1:], F32)
+        edge[1] = jnp.zeros(edge.shape[1:], BF16)
         near_token[1] = jnp.full((1, atom_rows), -tokens, jnp.int32)
 
     for name in ("out", "up", "down", "pool"):
@@ -588,16 +600,8 @@
         return jnp.where(lane < to + lanes - off, turned(tile), turned(tile + 1))
 
     def spread(copy_of):
-        def step(k, c):
-            target = far_first(k)
-
-            @pl.when(target != me)
-            def _():
-                copy_of(target, me).start()
-
-            return c
-
-        lax.fori_loop(0, n, step, 0)
+        for target in far_first():
+            copy_of(target, me).start()
 
     others = pl.ds(0, n - 1)
 
@@ -839,10 +843,10 @@
     exchange(*token_copy(), False)
     sent(
         remote(
-            stream.at[:, :, pl.ds(0, RIM), :], edge.at[0], edge_send.at[0], edge_recv.at[0, 0], right
+            rim.at[0], edge.at[0], edge_send.at[0], edge_recv.at[0, 0], right
         ),
         remote(
-            stream.at[:, :, pl.ds(0, RIM), :], edge.at[1], edge_send.at[1], edge_recv.at[0, 1], left
+            rim.at[1], edge.at[1], edge_send.at[1], edge_recv.at[0, 1], left
         ),
     )
     near_sel = [selects(near_token[side]).astype(BF16) for side in range(2)]
@@ -942,7 +946,8 @@
             pltpu.VMEM(w_coord.shape, F32),
             pltpu.VMEM(w_final.shape, BF16),
             pltpu.VMEM((GROUPS, gs, atom_rows, width), F32),
-            pltpu.VMEM((2, GROUPS, gs, RIM, width), F32),
+            pltpu.VMEM((2, GROUPS, gs, RIM, width), BF16),
+            pltpu.VMEM((2, GROUPS, gs, RIM, width), BF16),
             pltpu.VMEM((2, 1, atom_rows), jnp.int32),
             pltpu.VMEM((LAYERS, GROUPS, gs, atom_rows + 2 * RIM, 2 * width), BF16),
             pltpu.VMEM((GROUPS, gs * atom_rows, width), BF16),
@@ -992,7 +997,9 @@
             dma((2,)),
         ],
         compiler_params=pltpu.CompilerParams(
-            collective_id=0, has_side_effects=True, vmem_limit_bytes=56 * 1024 * 1024
+            collective_id=0,
+            has_side_effects=True,
+            vmem_limit_bytes=56 * 1024 * 1024,
         ),
     )(
         noise_level,

time: 43.3 us -> 42.8 us (0.988)
  Pallas kernels: 42.5 us -> 42 us
    pallas_call x1, Pallas kernels: 41.8 us -> 41.3 us  [shards(): pl.pallas_call(functools.partial(kernel, n), name='denoise', out_shape=(p...]
where the time goes in v7:
time: 42.8 us; the launch traced here: 42.6 us
  Pallas kernels  42 us (98%)
  between operations  0.65 us (2%)
    pallas_call x1, Pallas kernels, shards(): pl.pallas_call(functools.partial(kernel, n), name='denoise', out_shape=(p...  41.3 us

profile of v7, /device:TPU:1, one launch (start us, length us, event | category | flops | bytes accessed | tf_op | source)
XLA Modules:
  0.0 42.6 jit_solution(7611549920820341404)
XLA Ops:
  0.6 41.3 %denoise.1 = (f32[3,4,128]{2,1,0:T(4,128)S(1)}, f32[4,16,768]{2,1,0:T(8,128)S(1)}) custom-call(s32[4]{0:T(128)} %level_hbm.1, s32[2,4]{1,0:T(2,128)} %bitcast.5, f32[3,128]{1,0:T(4,128)} %x_true_hbm.1, f32[3,4,128]{2,1,0:T(4,128)} %bitcast.4, bf16[128,128]{1,0:T(8,128)(2,1)} %single_hbm.1, s32[1,128]{1,0:T(1,128)} %bitcast.6, f32[4,4,32,128]{3,2,1,0:T(8,128)} %bias_hbm.1, ...), custom_call_target="tpu_custom_call" | custom-call | tf_op jit(solution)/shard_map/denoise/pallas_call | solution.py:930
  41.9 0.7 %store.1 = (f32[3,4,128]{2,1,0:T(4,128)}, f32[4,16,768]{2,1,0:T(8,128)}) custom-call(f32[3,4,128]{2,1,0:T(4,128)S(1)} %get-tuple-element.6.denoised_ref, f32[4,16,768]{2,1,0:T(8,128)S(1)} %get-tuple-element.7.state_ref), custom_call_target="tpu_custom_call" | custom-call | tf_op jit(solution)/shard_map/store/pallas_call | solution.py:1025
